TPU v7x, 32 devices: a whole 2x2x4 slice. The times are simulated.
32 devices in a mesh: strip: 8 (over z, x), lev: 4 (over y, core).
Axes of the slice: x: 2, y: 2, z: 4, core: 2. Of those that a mesh axis runs over, the one named last changes fastest.
Arguments:
- cotangent: float32 [4, 256, 128, 128], P(None, 'lev', 'strip'), may hold values from -6 to 6
- blocks: float32 [4, 256, 64], P(None, 'lev'), may hold values from -0.25 to 1.3
- couple: float32 [4, 4, 128, 128], P(None, 'lev', 'strip'), may hold values from 0 to 1, as said below
- kappa: float32 [128, 128], P('strip'), may hold values from 0.05 to 0.24
Outputs:
- field_adjoint: float32 [4, 256, 128, 128], P(None, 'lev', 'strip')
Inputs may be any that keep to these rules, and one draw needn't show every extreme that they name: `couple`: coupling weights lie in 0 to 1.
All inputs are finite; a program needn't handle non-finite values.
Results may differ from a plain program's by a relative error of at most 0.0001.
Values sent between devices are 32-bit elements; how exact they have to be, the bound alone decides.
No kernel may reach another device: no remote copies, remote signals or barrier semaphores. Data moves between devices by JAX's collectives and lax.ppermute only.
A program may use at most 64 MiB of HBM per device.

v0:
```python
import jax
import jax.numpy as jnp
from jax import lax
from jax.sharding import PartitionSpec as P


def prefix(value, axis, join, neutral):
    count, mine = (lax.axis_size(axis), lax.axis_index(axis))
    pieces = jax.tree.map(lambda part: lax.all_gather(part, axis), value)
    pieces = jax.tree.map(lambda part: part[::-1], pieces)
    mine = count - 1 - mine
    total = jax.tree.map(
        lambda part, zero: jnp.full_like(part, 0) + jnp.asarray(zero, part.dtype), value, neutral
    )

    def lap(position, total):
        longer = join(total, jax.tree.map(lambda part: part[position], pieces))
        return jax.tree.map(lambda new, old: jnp.where(position < mine, new, old), longer, total)

    return lax.fori_loop(0, count - 1, lap, total)


def padded(block, sides, width):
    for axis, dim in sides:
        count = lax.axis_size(axis)
        forward = [(i, i + 1) for i in range(count - 1)]
        backward = [(target, source) for source, target in forward]
        low = lax.ppermute(
            lax.slice_in_dim(block, block.shape[dim] - width, None, axis=dim), axis, forward
        )
        high = lax.ppermute(lax.slice_in_dim(block, 0, width, axis=dim), axis, backward)
        block = jnp.concatenate([low, block, high], axis=dim)
    return block


def compose(earlier, later):
    return (later[0] * earlier[0], later[1] + later[0] * earlier[1])


def on_device(cotangent, blocks, couple, kappa):
    fields, levels, strip_rows, columns = cotangent.shape
    flattened = cotangent.reshape(fields, levels, strip_rows * columns)
    totals = jnp.sum(flattened, axis=1)
    retain = couple.reshape(fields, strip_rows * columns)
    own_offset = retain * totals
    unities = jnp.ones_like(retain)
    nothing = jnp.zeros_like(retain)
    carried = prefix((retain, own_offset), "lev", compose, (unities, nothing))[1]
    forced = flattened.at[:, -1, :].add(carried)
    adjoint = jnp.einsum("fkl,fkc->flc", blocks, forced, precision=lax.Precision.HIGHEST)
    adjoint = adjoint.reshape(fields, levels, strip_rows, columns)
    weighted = kappa * adjoint
    extended = padded(weighted, (("strip", 2),), 1)
    cross_strip_span = extended[:, :, 2:] + extended[:, :, :-2]
    padded_side = jnp.pad(weighted, ((0, 0), (0, 0), (0, 0), (1, 1)))
    along_strip = padded_side[..., 2:] + padded_side[..., :-2]
    return adjoint + cross_strip_span + along_strip - 4.0 * weighted


def solution(mesh):
    placed = (
        P(None, "lev", "strip", None),
        P(None, "lev", None),
        P(None, "lev", "strip", None),
        P("strip", None),
    )
    return jax.shard_map(
        on_device,
        mesh=mesh,
        in_specs=placed,
        out_specs=P(None, "lev", "strip", None),
        check_vma=False,
    )
```

profile of v0, /device:TPU:12, one launch (start us, length us, event | category | flops | bytes accessed | tf_op | source)
XLA Modules:
  0.0 36.7 jit_solution(14678197415944226728)
XLA Ops:
  0.0 0.0 copy-start
  0.0 0.8 %all_gather_reshape.3 = f32[1,4,2048]{2,1,0:T(4,128)S(1)} reshape(f32[4,1,16,128]{3,2,1,0:T(8,128)} %param.10) | data formatting | bytes 65536 | tf_op jit(solution)/shard_map/all_gather;reshape | solution.py:9
  0.8 0.0 copy-start.1
  0.8 2.9 %reshape.62 = f32[4,64,2048]{2,1,0:T(8,128)} reshape(f32[4,64,16,128]{3,2,1,0:T(8,128)} %param.8) | data formatting | bytes 4194304 | tf_op jit(solution)/shard_map/reshape | solution.py:42
  3.7 0.0 copy-done.1
  3.7 0.1 reduce_sum.11
  3.8 5.4 %all_gather.8 = f32[4,4,2048]{2,1,0:T(4,128)S(1)} all-gather(f32[1,4,2048]{2,1,0:T(4,128)S(1)} %all_gather_reshape.3), channel_id=1, replica_groups=mesh['strip'=8,'lev'=4] {'lev'}, dimensions={0}, use_global_device_ids=true | all-gather | bytes 163840 | tf_op jit(solution)/shard_map/all_gather | solution.py:9
  9.3 5.4 %all_gather.7 = f32[4,4,2048]{2,1,0:T(4,128)S(1)} all-gather(f32[1,4,2048]{2,1,0:T(4,128)S(1)} %mul.31), channel_id=1, replica_groups=mesh['strip'=8,'lev'=4] {'lev'}, dimensions={0}, use_global_device_ids=true | all-gather | bytes 163840 | tf_op jit(solution)/shard_map/all_gather | solution.py:9
  14.7 0.2 while.15
  14.9 2.9 %copy.15 = f32[4,64,2048]{2,0,1:T(4,128)S(1)} copy(f32[4,64,2048]{2,1,0:T(8,128)} %reshape.62) | data formatting | bytes 4194304 | tf_op jit(solution)/shard_map/reshape | solution.py:42
  17.8 0.0 copy-done
  17.8 0.0 copy-start.2
  17.9 3.3 %fusion.8 = f32[4,8,16,8,128]{4,3,2,1,0:T(8,128)S(1)} fusion(f32[4,64,64]{2,1,0:T(8,128)S(1)} %copy-done, f32[4,64,2048]{2,0,1:T(4,128)S(1)} %fusion.11), kind=kOutput, calls=%fused_computation.15 | convolution fusion | flops 402653184 | bytes 4259840 | tf_op jit(solution)/shard_map/fkl,fkc->flc/dot_general | solution.py:50
  21.1 0.0 copy-done.2
  21.2 0.3 bitcast_multiply_fusion.1
  21.5 3.3 %collective-permute-start = (f32[4,64,1,128]{3,1,2,0:T(8,128)S(1)}, f32[4,64,1,128]{3,1,2,0:T(8,128)S(1)}, u32[]{:S(2)}, u32[]{:S(2)}) collective-permute-start(f32[4,64,1,128]{3,1,2,0:T(8,128)S(1)} %get-tuple-element.140), channel_id=1, source_target_pairs={{4,0},{8,4},{12,8},{16,12},{20,16},{24,20},{28,24},{5,1},{9,5},{13... | collective-permute-start | bytes 393224 | tf_op jit(solution)/shard_map/ppermute | solution.py:31
  24.8 2.6 %collective-permute-start.1 = (f32[4,64,1,128]{3,1,2,0:T(8,128)S(1)}, f32[4,64,1,128]{3,1,2,0:T(8,128)S(1)}, u32[]{:S(2)}, u32[]{:S(2)}) collective-permute-start(f32[4,64,1,128]{3,1,2,0:T(8,128)S(1)} %get-tuple-element.141), channel_id=1, source_target_pairs={{0,4},{4,8},{8,12},{12,16},{16,20},{20,24},{24,28},{1,5},{5,9},{9,... | collective-permute-start | bytes 393224 | tf_op jit(solution)/shard_map/ppermute | solution.py:28
  27.3 1.8 %collective-permute-done = f32[4,64,1,128]{3,1,2,0:T(8,128)S(1)} collective-permute-done((f32[4,64,1,128]{3,1,2,0:T(8,128)S(1)}, f32[4,64,1,128]{3,1,2,0:T(8,128)S(1)}, u32[]{:S(2)}, u32[]{:S(2)}) %collective-permute-start) | collective-permute-done | bytes 131104 | tf_op jit(solution)/shard_map/ppermute | solution.py:31
  29.1 3.9 %collective-permute-done.1 = f32[4,64,1,128]{3,1,2,0:T(8,128)S(1)} collective-permute-done((f32[4,64,1,128]{3,1,2,0:T(8,128)S(1)}, f32[4,64,1,128]{3,1,2,0:T(8,128)S(1)}, u32[]{:S(2)}, u32[]{:S(2)}) %collective-permute-start.1) | collective-permute-done | bytes 131104 | tf_op jit(solution)/shard_map/ppermute | solution.py:28
  33.0 1.1 %fusion.4 = f32[4,64,16,128]{3,1,2,0:T(8,128)S(1)} fusion(f32[4,64,16,128]{3,1,2,0:T(8,128)S(1)} %bitcast_multiply_fusion.1, f32[4,64,1,128]{3,1,2,0:T(8,128)S(1)} %collective-permute-done.1, f32[4,64,1,128]{3,1,2,0:T(8,128)S(1)} %collective-permute-done, f32[4,8,16,8,128]{4,3,2,1,0:T(8,128)S(1)} %fusion.8), kind=kLoop, calls=%fused_computation.7 | loop fusion | flops 4194304 | bytes 6553600 | tf_op jit(solution)/shard_map/sub | solution.py:57
  34.2 2.5 %copy.13 = f32[4,64,16,128]{3,2,1,0:T(8,128)} copy(f32[4,64,16,128]{3,1,2,0:T(8,128)S(1)} %fusion.4) | data formatting | bytes 4194304 | tf_op jit(solution)/shard_map/sub | solution.py:57
  (10 shorter events, 0.2 us)
Async XLA Ops:
  0.0 17.8 %copy-start = (f32[4,64,64]{2,1,0:T(8,128)S(1)}, f32[4,64,64]{2,1,0:T(8,128)}, u32[]{:S(2)}) copy-start(f32[4,64,64]{2,1,0:T(8,128)} %param.9) | copy-start | bytes 196612
  0.8 2.9 %copy-start.1 = (f32[4,64,16,128]{3,2,1,0:T(8,128)S(1)}, f32[4,64,16,128]{3,2,1,0:T(8,128)}, u32[]{:S(2)}) copy-start(f32[4,64,16,128]{3,2,1,0:T(8,128)} %param.8) | copy-start | bytes 6291460
  17.8 3.3 %copy-start.2 = (f32[16,128]{1,0:T(8,128)S(1)}, f32[16,128]{1,0:T(8,128)}, u32[]{:S(2)}) copy-start(f32[16,128]{1,0:T(8,128)} %param.11) | copy-start | bytes 24580
  21.5 7.6 %collective-permute-start = (f32[4,64,1,128]{3,1,2,0:T(8,128)S(1)}, f32[4,64,1,128]{3,1,2,0:T(8,128)S(1)}, u32[]{:S(2)}, u32[]{:S(2)}) collective-permute-start(f32[4,64,1,128]{3,1,2,0:T(8,128)S(1)} %get-tuple-element.140), channel_id=1, source_target_pairs={{4,0},{8,4},{12,8},{16,12},{20,16},{24,20},{28,24},{5,1},{9,5},{13... | collective-permute-start | bytes 393224 | tf_op jit(solution)/shard_map/ppermute | solution.py:31
  24.8 8.3 %collective-permute-start.1 = (f32[4,64,1,128]{3,1,2,0:T(8,128)S(1)}, f32[4,64,1,128]{3,1,2,0:T(8,128)S(1)}, u32[]{:S(2)}, u32[]{:S(2)}) collective-permute-start(f32[4,64,1,128]{3,1,2,0:T(8,128)S(1)} %get-tuple-element.141), channel_id=1, source_target_pairs={{0,4},{4,8},{8,12},{12,16},{16,20},{20,24},{24,28},{1,5},{5,9},{9,... | collective-permute-start | bytes 393224 | tf_op jit(solution)/shard_map/ppermute | solution.py:28
where the time goes:
time: 37.2 us; the launch traced here: 36.7 us
  blocking collectives  10.8 us (29%)
  local copies, waits for them, and re-layouts  9.21 us (25%)
  starting transfers between devices  5.84 us (16%)
  waiting for transfers between devices  5.69 us (15%)
  matrix products  3.28 us (9%)
  other arithmetic  1.65 us (4%)
    all_gather x2, blocking collectives, prefix(): pieces = jax.tree.map(lambda part: lax.all_gather(part, axis), value)  10.8 us
    reshape x2, local copies, waits for them, and re-layouts, on_device(): flattened = cotangent.reshape(fields, levels, strip_rows * columns)  5.79 us
    ppermute x1, waiting for transfers between devices, padded(): lax.ppermute(lax.slice_in_dim(block, block.shape[dim] - width, None, axis...  3.91 us
    dot_general x1, matrix products, on_device(): jnp.einsum('fkl,fkc->flc', blocks, forced, precision=lax.Precision.HIGHEST)  3.28 us
    ppermute x1, starting transfers between devices, padded(): lax.ppermute(lax.slice_in_dim(block, 0, width, axis=dim), axis, backward)  3.28 us
    ppermute x1, starting transfers between devices, padded(): lax.ppermute(lax.slice_in_dim(block, block.shape[dim] - width, None, axis...  2.56 us
    sub x1, local copies, waits for them, and re-layouts, on_device(): return adjoint + cross_strip_span + along_strip - 4.0 * weighted  2.54 us
    ppermute x1, waiting for transfers between devices, padded(): lax.ppermute(lax.slice_in_dim(block, 0, width, axis=dim), axis, backward)  1.78 us
  transfers between devices with their start and end apart: 2, of which 2 were waited for; matrix products, arithmetic and copies ran while one was open for 0% of the time, Pallas kernels for 0%

commit v1 on v0

v1 whole, which is shorter than its diff:
```python
import functools

import jax
import jax.numpy as jnp
from jax import lax
from jax.experimental import pallas as pl
from jax.experimental.pallas import tpu as pltpu
from jax.sharding import PartitionSpec as P

VMEM = pl.BlockSpec(memory_space=pltpu.VMEM)
LIMIT = 16 * 1024 * 1024


def call(body, outs, cost, *args):
    return pl.pallas_call(
        body,
        out_shape=outs,
        in_specs=[VMEM] * len(args),
        out_specs=[VMEM] * len(outs),
        compiler_params=pltpu.CompilerParams(vmem_limit_bytes=LIMIT),
        cost_estimate=pl.CostEstimate(flops=cost[0], bytes_accessed=cost[1], transcendentals=0),
    )(*args)


def f32(*shape):
    return jax.ShapeDtypeStruct(shape, jnp.float32)


def halves(x):
    high = x.astype(jnp.bfloat16)
    low = (x - high.astype(jnp.float32)).astype(jnp.bfloat16)
    return high, low


def product(high, low, x):
    a, b = halves(x)
    dot = functools.partial(jnp.dot, preferred_element_type=jnp.float32)
    return dot(high, a) + (dot(high, b) + dot(low, a))


def pack_kernel(dims, cot, couple, kappa, first, second, pair):
    fields, levels, rows = dims
    even = lax.rem(lax.axis_index("strip"), 2) == 0
    for f in range(fields):
        base = f * levels * rows
        low = kappa[0:1, :] * cot[pl.ds(base, levels, stride=rows), :]
        high = kappa[rows - 1 : rows, :] * cot[pl.ds(base + rows - 1, levels, stride=rows), :]
        first[f * levels : (f + 1) * levels, :] = jnp.where(even, high, low)
        second[f * levels : (f + 1) * levels, :] = jnp.where(even, low, high)
        block = cot[base : base + levels * rows, :].reshape(levels, rows, -1)
        weight = couple[f * rows : (f + 1) * rows, :]
        pair[f * rows : (f + 1) * rows, :] = weight * jnp.sum(block, axis=0)
        pair[(fields + f) * rows : (fields + f + 1) * rows, :] = weight


def across(weighted):
    lane = lax.broadcasted_iota(jnp.int32, weighted.shape, 1)
    last = weighted.shape[1] - 1
    left = jnp.where(lane == 0, 0.0, pltpu.roll(weighted, 1, 1))
    right = jnp.where(lane == last, 0.0, pltpu.roll(weighted, last, 1))
    return left + right


def main_kernel(dims, cot, blocks, kappa, out, high_ref, low_ref):
    fields, levels, rows = dims
    for f in range(fields):
        high, low = halves(jnp.transpose(blocks[f]))
        high_ref[f], low_ref[f] = high, low
        base = f * levels * rows
        load = lambda x: cot[pl.ds(base + x, levels, stride=rows), :]
        scaled = lambda x, v: v * kappa[x : x + 1, :]
        before = None
        here = load(0)
        here_w = scaled(0, here)
        for x in range(rows):
            total = here - 4.0 * here_w + across(here_w)
            if before is not None:
                total = total + before
            if x + 1 < rows:
                after = load(x + 1)
                after_w = scaled(x + 1, after)
                total = total + after_w
            out[pl.ds(base + x, levels, stride=rows), :] = product(high, low, total)
            before, here, here_w = here_w, after, after_w


def carry_kernel(dims, count, *refs):
    fields, rows = dims
    kappa = refs[0]
    received = refs[1:count]
    spread, first, second = refs[count:]
    size = fields * rows
    mine = lax.axis_index("lev")
    even = lax.rem(lax.axis_index("strip"), 2) == 0
    carried = jnp.zeros((size, kappa.shape[1]), jnp.float32)
    for piece in range(count - 1, 0, -1):
        offset, weight = received[0][0:size, :], received[0][size:, :]
        for step in range(2, count):
            here = partner(mine, step, count) == piece
            offset = jnp.where(here, received[step - 1][0:size, :], offset)
            weight = jnp.where(here, received[step - 1][size:, :], weight)
        carried = jnp.where(piece > mine, offset + weight * carried, carried)
    tall = jnp.concatenate([kappa[...]] * fields, axis=0)
    weighted = tall * carried
    row = lax.rem(lax.broadcasted_iota(jnp.int32, weighted.shape, 0), rows)
    below = jnp.where(row == 0, 0.0, pltpu.roll(weighted, 1, 0))
    above = jnp.where(row == rows - 1, 0.0, pltpu.roll(weighted, size - 1, 0))
    spread[...] = carried - 4.0 * weighted + across(weighted) + below + above
    first[...] = jnp.zeros_like(first)
    second[...] = jnp.zeros_like(second)
    for f in range(fields):
        low = weighted[f * rows : f * rows + 1, :]
        high = weighted[(f + 1) * rows - 1 : (f + 1) * rows, :]
        first[f : f + 1, :] = jnp.where(even, high, low)
        second[f : f + 1, :] = jnp.where(even, low, high)


def final_kernel(dims, base_out, last, spread, high_ref, low_ref, near, far, near_c, far_c, out):
    fields, levels, rows = dims
    even = lax.rem(lax.axis_index("strip"), 2) == 0
    for f in range(fields):
        base = f * levels * rows
        piece = spread[f * rows : (f + 1) * rows, :]
        for l in range(levels):
            at = base + l * rows
            factor = last[f * levels + l : f * levels + l + 1, :]
            out[at : at + rows, :] = base_out[at : at + rows, :] + factor * piece
        near_f = near[f * levels : (f + 1) * levels, :]
        far_f = far[f * levels : (f + 1) * levels, :]
        top = lax.broadcasted_iota(jnp.int32, near_f.shape, 0) == levels - 1
        near_f = near_f + jnp.where(top, near_c[f : f + 1, :], 0.0)
        far_f = far_f + jnp.where(top, far_c[f : f + 1, :], 0.0)
        low = jnp.where(even, far_f, near_f)
        high = jnp.where(even, near_f, far_f)
        extra = product(high_ref[f], low_ref[f], jnp.concatenate([low, high], axis=1))
        columns = low.shape[1]
        for x, part in ((0, extra[:, :columns]), (rows - 1, extra[:, columns:])):
            at = pl.ds(base + x, levels, stride=rows)
            out[at, :] = out[at, :] + part


def partner(index, step, count):
    if count & (count - 1) == 0:
        return index ^ step
    return lax.rem(index + step, count)


def on_device(cotangent, blocks, couple, kappa):
    fields, levels, rows, columns = cotangent.shape
    pieces, strips = lax.axis_size("lev"), lax.axis_size("strip")
    dims = (fields, levels, rows)
    cot = cotangent.reshape(fields * levels * rows, columns)
    weights = couple.reshape(fields * rows, columns)
    edge = f32(fields * levels, columns)
    nbytes = 4 * cot.size

    first, second, pair = call(
        functools.partial(pack_kernel, dims),
        [edge, edge, f32(2 * fields * rows, columns)],
        (cot.size, nbytes),
        cot,
        weights,
        kappa,
    )
    one = [(i, i ^ 1) for i in range(strips) if i ^ 1 < strips]
    two = [(i, j) for i in range(strips) for j in [((i + 1) ^ 1) - 1] if 0 <= j < strips]
    near = lax.ppermute(first, "strip", one)
    far = lax.ppermute(second, "strip", two)
    received = []
    for step in range(1, pieces):
        if pieces & (pieces - 1) == 0:
            pairs = [(i, i ^ step) for i in range(pieces)]
        else:
            pairs = [((i + step) % pieces, i) for i in range(pieces)]
        received.append(lax.ppermute(pair, "lev", pairs))
    base_out, high, low = call(
        functools.partial(main_kernel, dims),
        [f32(*cot.shape)] + [jax.ShapeDtypeStruct((fields, levels, levels), jnp.bfloat16)] * 2,
        (6 * levels * cot.size, 2 * nbytes),
        cot,
        blocks,
        kappa,
    )
    tiny = f32(-(-fields // 8) * 8, columns)
    spread, first_c, second_c = call(
        functools.partial(carry_kernel, (fields, rows), pieces),
        [f32(fields * rows, columns), tiny, tiny],
        (weights.size * 10, weights.size * 32),
        kappa,
        *received,
    )
    near_c = lax.ppermute(first_c, "strip", one)
    far_c = lax.ppermute(second_c, "strip", two)
    last = jnp.broadcast_to(blocks[:, levels - 1, :].reshape(fields * levels, 1), (fields * levels, columns))
    (out,) = call(
        functools.partial(final_kernel, dims),
        [f32(*cot.shape)],
        (4 * cot.size, 2 * nbytes),
        base_out,
        last,
        spread,
        high,
        low,
        near,
        far,
        near_c,
        far_c,
    )
    return out.reshape(cotangent.shape)


def solution(mesh):
    placed = (
        P(None, "lev", "strip", None),
        P(None, "lev", None),
        P(None, "lev", "strip", None),
        P("strip", None),
    )
    return jax.shard_map(
        on_device,
        mesh=mesh,
        in_specs=placed,
        out_specs=P(None, "lev", "strip", None),
        check_vma=False,
    )
```

time: 37.2 us -> 21.2 us (0.57)
  blocking collectives: 10.8 us -> 0 us
  local copies, waits for them, and re-layouts: 9.21 us -> 3.96 us
  starting transfers between devices: 5.84 us -> 10.3 us
  Pallas kernels: 0 us -> 4.37 us
  waiting for transfers between devices: 5.69 us -> 2.11 us
  matrix products: 3.28 us -> 0 us
  other arithmetic: 1.65 us -> 0 us
    all_gather x2 -> x0, blocking collectives: 10.8 us -> none  [prefix(): pieces = jax.tree.map(lambda part: lax.all_gather(part, axis), value)]
    reshape x2 -> x0, local copies, waits for them, and re-layouts: 5.79 us -> none  [on_device(): flattened = cotangent.reshape(fields, levels, strip_rows * columns)]
    ppermute x2 -> x7, starting transfers between devices: 5.84 us -> 10.3 us  [the longest x1 2.68 us: on_device(): near_c = lax.ppermute(first_c, 'strip', one)]
    pallas_call x0 -> x4, Pallas kernels: none -> 4.37 us  [call(): pl.pallas_call(body, out_shape=outs, in_specs=[VMEM] * len(args), out_spe...]
    ppermute x2 -> x7, waiting for transfers between devices: 5.69 us -> 2.11 us  [the longest x1 2.1 us: on_device(): far_c = lax.ppermute(second_c, 'strip', two)]
    dot_general x1 -> x0, matrix products: 3.28 us -> none  [on_device(): jnp.einsum('fkl,fkc->flc', blocks, forced, precision=lax.Precision.HIGHEST)]
    unnamed x6 -> x10, local copies, waits for them, and re-layouts: 0.02 us -> 3.05 us
    sub x1 -> x0, local copies, waits for them, and re-layouts: 2.54 us -> none  [on_device(): return adjoint + cross_strip_span + along_strip - 4.0 * weighted]
  transfers between devices with their start and end apart: 2 -> 7, of which waited for: 2 -> 1; matrix products, arithmetic and copies ran while one was open for 0% -> 4% of each run, Pallas kernels for 0% -> 11%
where the time goes in v1:
time: 21.2 us; the launch traced here: 20.8 us
  starting transfers between devices  10.3 us (49%)
  Pallas kernels  4.37 us (21%)
  local copies, waits for them, and re-layouts  3.96 us (19%)
  waiting for transfers between devices  2.11 us (10%)
    pallas_call x4, Pallas kernels, call(): pl.pallas_call(body, out_shape=outs, in_specs=[VMEM] * len(args), out_spe...  4.37 us
    unnamed x10, local copies, waits for them, and re-layouts  3.05 us
    ppermute x1, starting transfers between devices, on_device(): near_c = lax.ppermute(first_c, 'strip', one)  2.68 us
    ppermute x1, starting transfers between devices, on_device(): far = lax.ppermute(second, 'strip', two)  2.32 us
    ppermute x1, waiting for transfers between devices, on_device(): far_c = lax.ppermute(second_c, 'strip', two)  2.1 us
    ppermute x3, starting transfers between devices, on_device(): received.append(lax.ppermute(pair, 'lev', pairs))  1.91 us
    ppermute x1, starting transfers between devices, on_device(): far_c = lax.ppermute(second_c, 'strip', two)  1.91 us
    ppermute x1, starting transfers between devices, on_device(): near = lax.ppermute(first, 'strip', one)  1.49 us
  transfers between devices with their start and end apart: 7, of which 1 were waited for; matrix products, arithmetic and copies ran while one was open for 4% of the time, Pallas kernels for 11%

profile of v1, /device:TPU:12, one launch (start us, length us, event | category | flops | bytes accessed | tf_op | source)
XLA Modules:
  0.0 20.8 jit_solution(7507660406059659854)
XLA Ops:
  0.0 1.6 %copy-done = f32[4,64,16,128]{3,2,1,0:T(8,128)S(1)} copy-done((f32[4,64,16,128]{3,2,1,0:T(8,128)S(1)}, f32[4,64,16,128]{3,2,1,0:T(8,128)}, u32[]{:S(2)}) %copy-start) | copy-done | bytes 2097176
  1.6 0.7 %copy-done.3 = f32[16,128]{1,0:T(8,128)S(1)} copy-done((f32[16,128]{1,0:T(8,128)S(1)}, f32[16,128]{1,0:T(8,128)}, u32[]{:S(2)}) %copy-start.3) | copy-done | bytes 8216
  2.3 0.8 %copy-done.4 = f32[4,1,16,128]{3,2,1,0:T(8,128)S(1)} copy-done((f32[4,1,16,128]{3,2,1,0:T(8,128)S(1)}, f32[4,1,16,128]{3,2,1,0:T(8,128)}, u32[]{:S(2)}) %copy-start.4) | copy-done | bytes 32792
  3.1 0.2 %shard_map.47 = (f32[256,128]{1,0:T(8,128)S(1)}, f32[256,128]{1,0:T(8,128)S(1)}, f32[128,128]{1,0:T(8,128)S(1)}) custom-call(f32[4096,128]{1,0:T(8,128)S(1)} %bitcast.3, f32[64,128]{1,0:T(8,128)S(1)} %bitcast.5, f32[16,128]{1,0:T(8,128)S(1)} %copy-done.3), custom_call_target="tpu_custom_call" | custom-call | flops 524288 | bytes 2097152 | tf_op jit(solution)/shard_map/pallas_call | solution.py:15
  3.3 0.1 collective-permute-start.2
  3.3 1.5 %collective-permute-start.1 = (f32[128,128]{1,0:T(8,128)S(1)}, f32[128,128]{1,0:T(8,128)S(1)}, u32[]{:S(2)}, u32[]{:S(2)}) collective-permute-start(f32[128,128]{1,0:T(8,128)S(1)} %get-tuple-element.15), channel_id=1, source_target_pairs={{0,2},{1,3},{2,0},{3,1},{4,6},{5,7},{6,4},{7,5},{8,10},{9,11},{10,... | collective-permute-start | bytes 196616 | tf_op jit(solution)/shard_map/ppermute | solution.py:175
  4.8 0.4 %collective-permute-start = (f32[128,128]{1,0:T(8,128)S(1)}, f32[128,128]{1,0:T(8,128)S(1)}, u32[]{:S(2)}, u32[]{:S(2)}) collective-permute-start(f32[128,128]{1,0:T(8,128)S(1)} %get-tuple-element.15), channel_id=1, source_target_pairs={{0,1},{1,0},{2,3},{3,2},{4,5},{5,4},{6,7},{7,6},{8,9},{9,8},{10,11... | collective-permute-start | bytes 196616 | tf_op jit(solution)/shard_map/ppermute | solution.py:175
  5.2 1.5 %collective-permute-start.3 = (f32[256,128]{1,0:T(8,128)S(1)}, f32[256,128]{1,0:T(8,128)S(1)}, u32[]{:S(2)}, u32[]{:S(2)}) collective-permute-start(f32[256,128]{1,0:T(8,128)S(1)} %get-tuple-element.19), channel_id=1, source_target_pairs={{0,4},{4,0},{8,12},{12,8},{16,20},{20,16},{24,28},{28,24},{1,5},{5... | collective-permute-start | bytes 393224 | tf_op jit(solution)/shard_map/ppermute | solution.py:167
  6.7 2.3 %collective-permute-start.4 = (f32[256,128]{1,0:T(8,128)S(1)}, f32[256,128]{1,0:T(8,128)S(1)}, u32[]{:S(2)}, u32[]{:S(2)}) collective-permute-start(f32[256,128]{1,0:T(8,128)S(1)} %get-tuple-element.20), channel_id=1, source_target_pairs={{4,8},{8,4},{12,16},{16,12},{20,24},{24,20},{5,9},{9,5},{13,17},{1... | collective-permute-start | bytes 393224 | tf_op jit(solution)/shard_map/ppermute | solution.py:168
  9.0 0.7 %slice_reduce_fusion = f32[4,64]{1,0:T(4,128)S(1)} fusion(f32[4,64,64]{2,1,0:T(8,128)} %blocks.1), kind=kLoop, calls=%fused_computation | loop fusion | bytes 2048 | tf_op jit(solution)/shard_map/slice | solution.py:194
  9.7 0.0 collective-permute-done.2.refs_3_
  9.8 0.0 collective-permute-done.1.refs_2_
  9.8 0.0 collective-permute-done.refs_1_
  9.8 0.1 shard_map.48
  9.9 2.7 %collective-permute-start.5 = (f32[8,128]{1,0:T(8,128)S(1)}, f32[8,128]{1,0:T(8,128)S(1)}, u32[]{:S(2)}, u32[]{:S(2)}) collective-permute-start(f32[8,128]{1,0:T(8,128)S(1)} %get-tuple-element.21), channel_id=1, source_target_pairs={{0,4},{4,0},{8,12},{12,8},{16,20},{20,16},{24,28},{28,24},{1,5},{5... | collective-permute-start | bytes 12296 | tf_op jit(solution)/shard_map/ppermute | solution.py:192
  12.6 1.9 %collective-permute-start.6 = (f32[8,128]{1,0:T(8,128)S(1)}, f32[8,128]{1,0:T(8,128)S(1)}, u32[]{:S(2)}, u32[]{:S(2)}) collective-permute-start(f32[8,128]{1,0:T(8,128)S(1)} %get-tuple-element.22), channel_id=1, source_target_pairs={{4,8},{8,4},{12,16},{16,12},{20,24},{24,20},{5,9},{9,5},{13,17},{1... | collective-permute-start | bytes 12296 | tf_op jit(solution)/shard_map/ppermute | solution.py:193
  14.5 2.3 %shard_map.46 = (f32[4096,128]{1,0:T(8,128)S(1)}, bf16[4,64,64]{2,1,0:T(8,128)(2,1)S(1)}, bf16[4,64,64]{2,1,0:T(8,128)(2,1)S(1)}) custom-call(f32[4096,128]{1,0:T(8,128)S(1)} %bitcast.4, f32[4,64,64]{2,1,0:T(8,128)S(1)} %copy-done.2, f32[16,128]{1,0:T(8,128)S(1)} %copy-done.3), custom_call_target="tpu_custom_call" | custom-call | flops 201326592 | bytes 4194304 | tf_op jit(solution)/shard_map/pallas_call | solution.py:15
  16.8 0.1 broadcast_in_dim.7
  16.9 0.0 collective-permute-done.5.near_c
  16.9 2.1 %collective-permute-done.6.far_c = f32[8,128]{1,0:T(8,128)S(1)} collective-permute-done((f32[8,128]{1,0:T(8,128)S(1)}, f32[8,128]{1,0:T(8,128)S(1)}, u32[]{:S(2)}, u32[]{:S(2)}) %collective-permute-start.6) | collective-permute-done | bytes 4128 | tf_op jit(solution)/shard_map/ppermute | solution.py:193
  19.0 0.0 collective-permute-done.3.near
  19.0 0.0 collective-permute-done.4.far
  19.0 0.1 broadcast_in_dim.8.last
  19.1 1.8 %shard_map.49 = f32[4096,128]{1,0:T(8,128)} custom-call(f32[4096,128]{1,0:T(8,128)S(1)} %get-tuple-element.14.base_out, f32[256,128]{1,0:T(8,128)S(1)} %broadcast_in_dim.8.last, f32[64,128]{1,0:T(8,128)S(1)} %get-tuple-element.16.spread, bf16[4,64,64]{2,1,0:T(8,128)(2,1)S(1)} %get-tuple-element.17.high_ref, ...), custom_call_target="tpu_custom_call" | custom-call | flops 2097152 | bytes 4194304 | tf_op jit(solution)/shard_map/pallas_call | solution.py:15
  (7 shorter events, 0.0 us)
Async XLA Ops:
  0.0 1.6 %copy-start = (f32[4,64,16,128]{3,2,1,0:T(8,128)S(1)}, f32[4,64,16,128]{3,2,1,0:T(8,128)}, u32[]{:S(2)}) copy-start(f32[4,64,16,128]{3,2,1,0:T(8,128)} %param.4) | copy-start | bytes 6291460
  1.6 0.7 %copy-start.3 = (f32[16,128]{1,0:T(8,128)S(1)}, f32[16,128]{1,0:T(8,128)}, u32[]{:S(2)}) copy-start(f32[16,128]{1,0:T(8,128)} %refs_0_.1) | copy-start | bytes 24580
  2.3 0.8 %copy-start.4 = (f32[4,1,16,128]{3,2,1,0:T(8,128)S(1)}, f32[4,1,16,128]{3,2,1,0:T(8,128)}, u32[]{:S(2)}) copy-start(f32[4,1,16,128]{3,2,1,0:T(8,128)} %param.6) | copy-start | bytes 98308
  3.0 11.5 %copy-start.1 = (f32[4,64,16,128]{3,2,1,0:T(8,128)S(1)}, f32[4,64,16,128]{3,2,1,0:T(8,128)}, u32[]{:S(2)}) copy-start(f32[4,64,16,128]{3,2,1,0:T(8,128)} %param.4) | copy-start | bytes 6291460
  3.0 11.5 %copy-start.2 = (f32[4,64,64]{2,1,0:T(8,128)S(1)}, f32[4,64,64]{2,1,0:T(8,128)}, u32[]{:S(2)}) copy-start(f32[4,64,64]{2,1,0:T(8,128)} %blocks.1) | copy-start | bytes 196612
  3.3 6.5 %collective-permute-start.2 = (f32[128,128]{1,0:T(8,128)S(1)}, f32[128,128]{1,0:T(8,128)S(1)}, u32[]{:S(2)}, u32[]{:S(2)}) collective-permute-start(f32[128,128]{1,0:T(8,128)S(1)} %get-tuple-element.15), channel_id=1, source_target_pairs={{0,3},{1,2},{2,1},{3,0},{4,7},{5,6},{6,5},{7,4},{8,11},{9,10},{10,... | collective-permute-start | bytes 196616 | tf_op jit(solution)/shard_map/ppermute | solution.py:175
  3.3 6.4 %collective-permute-start.1 = (f32[128,128]{1,0:T(8,128)S(1)}, f32[128,128]{1,0:T(8,128)S(1)}, u32[]{:S(2)}, u32[]{:S(2)}) collective-permute-start(f32[128,128]{1,0:T(8,128)S(1)} %get-tuple-element.15), channel_id=1, source_target_pairs={{0,2},{1,3},{2,0},{3,1},{4,6},{5,7},{6,4},{7,5},{8,10},{9,11},{10,... | collective-permute-start | bytes 196616 | tf_op jit(solution)/shard_map/ppermute | solution.py:175
  4.8 5.0 %collective-permute-start = (f32[128,128]{1,0:T(8,128)S(1)}, f32[128,128]{1,0:T(8,128)S(1)}, u32[]{:S(2)}, u32[]{:S(2)}) collective-permute-start(f32[128,128]{1,0:T(8,128)S(1)} %get-tuple-element.15), channel_id=1, source_target_pairs={{0,1},{1,0},{2,3},{3,2},{4,5},{5,4},{6,7},{7,6},{8,9},{9,8},{10,11... | collective-permute-start | bytes 196616 | tf_op jit(solution)/shard_map/ppermute | solution.py:175
  5.2 13.8 %collective-permute-start.3 = (f32[256,128]{1,0:T(8,128)S(1)}, f32[256,128]{1,0:T(8,128)S(1)}, u32[]{:S(2)}, u32[]{:S(2)}) collective-permute-start(f32[256,128]{1,0:T(8,128)S(1)} %get-tuple-element.19), channel_id=1, source_target_pairs={{0,4},{4,0},{8,12},{12,8},{16,20},{20,16},{24,28},{28,24},{1,5},{5... | collective-permute-start | bytes 393224 | tf_op jit(solution)/shard_map/ppermute | solution.py:167
  6.7 12.3 %collective-permute-start.4 = (f32[256,128]{1,0:T(8,128)S(1)}, f32[256,128]{1,0:T(8,128)S(1)}, u32[]{:S(2)}, u32[]{:S(2)}) collective-permute-start(f32[256,128]{1,0:T(8,128)S(1)} %get-tuple-element.20), channel_id=1, source_target_pairs={{4,8},{8,4},{12,16},{16,12},{20,24},{24,20},{5,9},{9,5},{13,17},{1... | collective-permute-start | bytes 393224 | tf_op jit(solution)/shard_map/ppermute | solution.py:168
  9.9 7.0 %collective-permute-start.5 = (f32[8,128]{1,0:T(8,128)S(1)}, f32[8,128]{1,0:T(8,128)S(1)}, u32[]{:S(2)}, u32[]{:S(2)}) collective-permute-start(f32[8,128]{1,0:T(8,128)S(1)} %get-tuple-element.21), channel_id=1, source_target_pairs={{0,4},{4,0},{8,12},{12,8},{16,20},{20,16},{24,28},{28,24},{1,5},{5... | collective-permute-start | bytes 12296 | tf_op jit(solution)/shard_map/ppermute | solution.py:192
  12.6 6.4 %collective-permute-start.6 = (f32[8,128]{1,0:T(8,128)S(1)}, f32[8,128]{1,0:T(8,128)S(1)}, u32[]{:S(2)}, u32[]{:S(2)}) collective-permute-start(f32[8,128]{1,0:T(8,128)S(1)} %get-tuple-element.22), channel_id=1, source_target_pairs={{4,8},{8,4},{12,16},{16,12},{20,24},{24,20},{5,9},{9,5},{13,17},{1... | collective-permute-start | bytes 12296 | tf_op jit(solution)/shard_map/ppermute | solution.py:193

commit v2 on v1

v2 whole, which is shorter than its diff:
```python
import functools

import jax
import jax.numpy as jnp
from jax import lax
from jax.experimental import pallas as pl
from jax.experimental.pallas import tpu as pltpu
from jax.sharding import PartitionSpec as P

VMEM = pl.BlockSpec(memory_space=pltpu.VMEM)
HBM = pl.BlockSpec(memory_space=pltpu.HBM)
LIMIT = 16 * 1024 * 1024


def call(body, outs, cost, *args, ins=None, out_specs=None, scratch=()):
    return pl.pallas_call(
        body,
        out_shape=outs,
        in_specs=ins or [VMEM] * len(args),
        out_specs=out_specs or [VMEM] * len(outs),
        scratch_shapes=list(scratch),
        compiler_params=pltpu.CompilerParams(vmem_limit_bytes=LIMIT),
        cost_estimate=pl.CostEstimate(flops=cost[0], bytes_accessed=cost[1], transcendentals=0),
    )(*args)


def f32(*shape):
    return jax.ShapeDtypeStruct(shape, jnp.float32)


def halves(x):
    high = x.astype(jnp.bfloat16)
    low = (x - high.astype(jnp.float32)).astype(jnp.bfloat16)
    return high, low


def product(high, low, x):
    a, b = halves(x)
    dot = functools.partial(jnp.dot, preferred_element_type=jnp.float32)
    return dot(high, a) + (dot(high, b) + dot(low, a))


def even_strip():
    return lax.rem(lax.axis_index("strip"), 2) == 0


def pack_kernel(
    dims, cot_hbm, couple_hbm, kappa_hbm, cot, kappa, first, second, pair, couple, sems
):
    fields, levels, rows = dims
    chunk = levels * rows
    small = [
        pltpu.make_async_copy(kappa_hbm, kappa, sems.at[fields]),
        pltpu.make_async_copy(couple_hbm, couple, sems.at[fields + 1]),
    ]
    large = [
        pltpu.make_async_copy(
            cot_hbm.at[pl.ds(f * chunk, chunk)], cot.at[pl.ds(f * chunk, chunk)], sems.at[f]
        )
        for f in range(fields)
    ]
    for copy in small + large:
        copy.start()
    for copy in small:
        copy.wait()
    even = even_strip()
    for f in range(fields):
        large[f].wait()
        base = f * chunk
        low = kappa[0:1, :] * cot[pl.ds(base, levels, stride=rows), :]
        high = kappa[rows - 1 : rows, :] * cot[pl.ds(base + rows - 1, levels, stride=rows), :]
        first[f * levels : (f + 1) * levels, :] = jnp.where(even, high, low)
        second[f * levels : (f + 1) * levels, :] = jnp.where(even, low, high)
        block = cot[base : base + chunk, :].reshape(levels, rows, -1)
        weight = couple[f * rows : (f + 1) * rows, :]
        pair[f * rows : (f + 1) * rows, :] = weight * jnp.sum(block, axis=0)
        pair[(fields + f) * rows : (fields + f + 1) * rows, :] = weight


def chip_pair(mine, own, other, size):
    bottom = lax.rem(mine, 2) == 0
    offset = (own[0:size, :], other[0:size, :])
    weight = (own[size:, :], other[size:, :])
    order = lambda v: (jnp.where(bottom, v[0], v[1]), jnp.where(bottom, v[1], v[0]))
    return order(offset), order(weight)


def compose_kernel(own, other, chip):
    size = own.shape[0] // 2
    offset, weight = chip_pair(lax.axis_index("lev"), own, other, size)
    chip[0:size, :] = offset[0] + weight[0] * offset[1]
    if chip.shape[0] > size:
        chip[size:, :] = weight[0] * weight[1]


def across(weighted):
    lane = lax.broadcasted_iota(jnp.int32, weighted.shape, 1)
    last = weighted.shape[1] - 1
    left = jnp.where(lane == 0, 0.0, pltpu.roll(weighted, 1, 1))
    right = jnp.where(lane == last, 0.0, pltpu.roll(weighted, last, 1))
    return left + right


def carry_kernel(dims, chips, kappa, own, other, *refs):
    fields, _, rows = dims
    received = refs[: chips - 1]
    spread, first, second = refs[chips - 1 :]
    size = fields * rows
    mine = lax.axis_index("lev")
    my_chip = lax.div(mine, 2)
    offset, weight = chip_pair(mine, own, other, size)
    entry = jnp.zeros((size, kappa.shape[1]), jnp.float32)
    for chip in range(chips - 1, 0, -1):
        value, factor = received[0][0:size, :], received[0][size:, :] if chips > 2 else None
        for step in range(2, chips):
            here = partner(my_chip, step, chips) == chip
            value = jnp.where(here, received[step - 1][0:size, :], value)
            factor = jnp.where(here, received[step - 1][size:, :], factor)
        longer = value if chip == chips - 1 else value + factor * entry
        entry = jnp.where(chip > my_chip, longer, entry)
    carried = jnp.where(lax.rem(mine, 2) == 0, offset[1] + weight[1] * entry, entry)
    weighted = jnp.concatenate([kappa[...]] * fields, axis=0) * carried
    row = lax.rem(lax.broadcasted_iota(jnp.int32, weighted.shape, 0), rows)
    below = jnp.where(row == 0, 0.0, pltpu.roll(weighted, 1, 0))
    above = jnp.where(row == rows - 1, 0.0, pltpu.roll(weighted, size - 1, 0))
    spread[...] = carried - 4.0 * weighted + across(weighted) + below + above
    first[...] = jnp.zeros_like(first)
    second[...] = jnp.zeros_like(second)
    even = even_strip()
    for f in range(fields):
        low = weighted[f * rows : f * rows + 1, :]
        high = weighted[(f + 1) * rows - 1 : (f + 1) * rows, :]
        first[f : f + 1, :] = jnp.where(even, high, low)
        second[f : f + 1, :] = jnp.where(even, low, high)


def main_kernel(dims, cot, blocks, kappa, spread, out, high_ref, low_ref):
    fields, levels, rows = dims
    top = lax.broadcasted_iota(jnp.int32, (levels, kappa.shape[1]), 0) == levels - 1
    for f in range(fields):
        high, low = halves(jnp.transpose(blocks[f]))
        high_ref[f], low_ref[f] = high, low
        base = f * levels * rows
        load = lambda x: cot[pl.ds(base + x, levels, stride=rows), :]
        scaled = lambda x, v: v * kappa[x : x + 1, :]
        before = None
        here = load(0)
        here_w = scaled(0, here)
        for x in range(rows):
            total = here - 4.0 * here_w + across(here_w)
            if before is not None:
                total = total + before
            if x + 1 < rows:
                after = load(x + 1)
                after_w = scaled(x + 1, after)
                total = total + after_w
            total = total + jnp.where(top, spread[f * rows + x : f * rows + x + 1, :], 0.0)
            out[pl.ds(base + x, levels, stride=rows), :] = product(high, low, total)
            before, here, here_w = here_w, after, after_w


def final_kernel(dims, strips, base_out, high, low, near, far, near_c, far_c, out_hbm, out, sems):
    fields, levels, rows = dims
    chunk = levels * rows
    columns = near.shape[1]
    mine = lax.axis_index("strip")
    even = even_strip()
    has_near = jnp.logical_or(jnp.logical_not(even), mine + 1 < strips)
    has_far = jnp.where(even, mine > 0, mine + 1 < strips)
    top = lax.broadcasted_iota(jnp.int32, (levels, columns), 0) == levels - 1
    copies = []
    for f in range(fields):
        base = f * chunk
        out[base : base + chunk, :] = base_out[base : base + chunk, :]
        sides = []
        for here, halo, halo_c in ((has_near, near, near_c), (has_far, far, far_c)):
            value = halo[f * levels : (f + 1) * levels, :]
            value = value + jnp.where(top, halo_c[f : f + 1, :], 0.0)
            sides.append(jnp.where(here, value, 0.0))
        below = jnp.where(even, sides[1], sides[0])
        above = jnp.where(even, sides[0], sides[1])
        extra = product(high[f], low[f], jnp.concatenate([below, above], axis=1))
        for x, part in ((0, extra[:, :columns]), (rows - 1, extra[:, columns:])):
            at = pl.ds(base + x, levels, stride=rows)
            out[at, :] = out[at, :] + part
        span = pl.ds(base, chunk)
        copies.append(pltpu.make_async_copy(out.at[span], out_hbm.at[span], sems.at[f]))
        copies[-1].start()
    for copy in copies:
        copy.wait()


def partner(index, step, count):
    if count & (count - 1) == 0:
        return index ^ step
    return lax.rem(index + step, count)


def sources(step, count):
    if count & (count - 1) == 0:
        return [i ^ step for i in range(count)]
    return [(i + step) % count for i in range(count)]


def swaps(strips, pieces, shift):
    pairs = []
    for strip in range(strips):
        other = ((strip + shift) ^ 1) - shift
        for piece in range(pieces):
            mine = strip * pieces + piece
            inside = 0 <= other < strips
            pairs.append((mine, other * pieces + piece if inside else mine ^ 1))
    return pairs


def compute(cotangent, blocks, couple, kappa):
    fields, levels, rows, columns = cotangent.shape
    pieces, strips = lax.axis_size("lev"), lax.axis_size("strip")
    chips = pieces // 2
    dims = (fields, levels, rows)
    cot = cotangent.reshape(fields * levels * rows, columns)
    size = fields * rows
    edge = f32(fields * levels, columns)
    nbytes = 4 * cot.size
    square = jax.ShapeDtypeStruct((fields, levels, levels), jnp.bfloat16)
    tiny = f32(-(-fields // 8) * 8, columns)
    whole = ("strip", "lev")
    one, two = swaps(strips, pieces, 0), swaps(strips, pieces, 1)

    cot, kappa, first, second, pair = call(
        functools.partial(pack_kernel, dims),
        [f32(*cot.shape), f32(rows, columns), edge, edge, f32(2 * size, columns)],
        (cot.size, nbytes),
        *(
            pltpu.with_memory_space_constraint(x, pltpu.HBM)
            for x in (cot, couple.reshape(size, columns), kappa)
        ),
        ins=[HBM] * 3,
        scratch=[pltpu.VMEM((size, columns), jnp.float32), pltpu.SemaphoreType.DMA((fields + 2,))],
    )
    other = lax.ppermute(pair, "lev", [(i, i ^ 1) for i in range(pieces)])
    near = lax.ppermute(first, whole, one)
    (chip,) = call(
        compose_kernel, [f32(size * (2 if chips > 2 else 1), columns)], (4 * size, 16 * size), pair, other
    )
    received = []
    for step in range(1, chips):
        moves = [(2 * s + c, 2 * i + c) for i, s in enumerate(sources(step, chips)) for c in range(2)]
        received.append(lax.ppermute(chip, "lev", moves))
    far = lax.ppermute(second, whole, two)
    spread, first, second = call(
        functools.partial(carry_kernel, dims, chips),
        [f32(size, columns), tiny, tiny],
        (size * columns * 10, size * columns * 32),
        kappa,
        pair,
        other,
        *received,
    )
    far_c = lax.ppermute(second, whole, two)
    near_c = lax.ppermute(first, whole, one)
    base_out, high, low = call(
        functools.partial(main_kernel, dims),
        [f32(*cot.shape), square, square],
        (6 * levels * cot.size, 2 * nbytes),
        cot,
        blocks,
        kappa,
        spread,
    )
    (out,) = call(
        functools.partial(final_kernel, dims, strips),
        [f32(*cot.shape)],
        (4 * cot.size, 2 * nbytes),
        base_out,
        high,
        low,
        near,
        far,
        near_c,
        far_c,
        out_specs=[HBM],
        scratch=[pltpu.VMEM(cot.shape, jnp.float32), pltpu.SemaphoreType.DMA((fields,))],
    )
    return out.reshape(cotangent.shape)


def solution(mesh):
    placed = (
        P(None, "lev", "strip", None),
        P(None, "lev", None),
        P(None, "lev", "strip", None),
        P("strip", None),
    )
    return jax.shard_map(
        compute,
        mesh=mesh,
        in_specs=placed,
        out_specs=P(None, "lev", "strip", None),
        check_vma=False,
    )
```

time: 21.2 us -> 18 us (0.85); the launches traced: 20.8 us -> 17.9 us
  starting transfers between devices: 10.3 us -> 4.82 us
  waiting for transfers between devices: 2.11 us -> 7.23 us
  local copies, waits for them, and re-layouts: 3.96 us -> 0.01 us
  Pallas kernels: 4.37 us -> 5.77 us
    ppermute x7 -> x6, starting transfers between devices: 10.3 us -> 4.82 us  [the longest x1 2.68 us: compute(): near_c = lax.ppermute(first, whole, one)]
    ppermute x7 -> x6, waiting for transfers between devices: 2.11 us -> 7.23 us  [the longest x1 3.83 us: compute(): received.append(lax.ppermute(chip, 'lev', moves))]
    unnamed x10 -> x2, local copies, waits for them, and re-layouts: 3.05 us -> 0.01 us
    pallas_call x4 -> x5, Pallas kernels: 4.37 us -> 5.77 us  [call(): pl.pallas_call(body, out_shape=outs, in_specs=ins or [VMEM] * len(args),...]
    slice x1 -> x0, local copies, waits for them, and re-layouts: 0.74 us -> none  [on_device(): blocks[:, levels - 1, :].reshape(fields * levels, 1)]
  transfers between devices with their start and end apart: 7 -> 6, of which waited for: 1 -> 3; matrix products, arithmetic and copies ran while one was open for 4% -> 0% of each run, Pallas kernels for 11% -> 14%
where the time goes in v2:
time: 18 us; the launch traced here: 17.9 us
  waiting for transfers between devices  7.23 us (40%)
  Pallas kernels  5.77 us (32%)
  starting transfers between devices  4.82 us (27%)
    pallas_call x5, Pallas kernels, call(): pl.pallas_call(body, out_shape=outs, in_specs=ins or [VMEM] * len(args),...  5.77 us
    ppermute x1, waiting for transfers between devices, compute(): received.append(lax.ppermute(chip, 'lev', moves))  3.83 us
    ppermute x1, starting transfers between devices, compute(): near_c = lax.ppermute(first, whole, one)  2.68 us
    ppermute x1, waiting for transfers between devices, compute(): far_c = lax.ppermute(second, whole, two)  2.14 us
    ppermute x1, starting transfers between devices, compute(): near = lax.ppermute(first, whole, one)  1.56 us
    ppermute x1, waiting for transfers between devices, compute(): other = lax.ppermute(pair, 'lev', [(i, i ^ 1) for i in range(pieces)])  1.25 us
    ppermute x1, starting transfers between devices, compute(): far = lax.ppermute(second, whole, two)  0.42 us
  transfers between devices with their start and end apart: 6, of which 3 were waited for; matrix products, arithmetic and copies ran while one was open for 0% of the time, Pallas kernels for 14%

profile of v2, /device:TPU:12, one launch (start us, length us, event | category | flops | bytes accessed | tf_op | source)
XLA Modules:
  0.0 17.9 jit_solution(7107519902204877362)
XLA Ops:
  0.0 0.0 copy-start
  0.0 1.7 %shard_map.46 = (f32[4096,128]{1,0:T(8,128)S(1)}, f32[16,128]{1,0:T(8,128)S(1)}, f32[256,128]{1,0:T(8,128)S(1)}, f32[256,128]{1,0:T(8,128)S(1)}, f32[128,128]{1,0:T(8,128)S(1)}) custom-call(f32[4096,128]{1,0:T(8,128)} %bitcast.3, f32[64,128]{1,0:T(8,128)} %bitcast.4, f32[16,128]{1,0:T(8,128)} %kappa_hbm.1), custom_call_target="tpu_custom_call" | custom-call | flops 524288 | bytes 2097152 | tf_op jit(solution)/shard_map/pallas_call | solution.py:16
  1.7 1.6 %collective-permute-start.2 = (f32[256,128]{1,0:T(8,128)S(1)}, f32[256,128]{1,0:T(8,128)S(1)}, u32[]{:S(2)}, u32[]{:S(2)}) collective-permute-start(f32[256,128]{1,0:T(8,128)S(1)} %get-tuple-element.23), channel_id=1, source_target_pairs={{0,4},{1,5},{2,6},{3,7},{4,0},{5,1},{6,2},{7,3},{8,12},{9,13},{10,... | collective-permute-start | bytes 393224 | tf_op jit(solution)/shard_map/ppermute | solution.py:242
  3.3 0.4 %collective-permute-start.3 = (f32[256,128]{1,0:T(8,128)S(1)}, f32[256,128]{1,0:T(8,128)S(1)}, u32[]{:S(2)}, u32[]{:S(2)}) collective-permute-start(f32[256,128]{1,0:T(8,128)S(1)} %get-tuple-element.24), channel_id=1, source_target_pairs={{0,1},{1,0},{2,3},{3,2},{4,8},{5,9},{6,10},{7,11},{8,4},{9,5},{10,... | collective-permute-start | bytes 393224 | tf_op jit(solution)/shard_map/ppermute | solution.py:250
  3.7 0.0 collective-permute-start
  3.7 1.3 %collective-permute-done.other = f32[128,128]{1,0:T(8,128)S(1)} collective-permute-done((f32[128,128]{1,0:T(8,128)S(1)}, f32[128,128]{1,0:T(8,128)S(1)}, u32[]{:S(2)}, u32[]{:S(2)}) %collective-permute-start) | collective-permute-done | bytes 65568 | tf_op jit(solution)/shard_map/ppermute | solution.py:241
  5.0 0.2 collective-permute-start.1
  5.1 3.8 %collective-permute-done.1.refs_0_ = f32[64,128]{1,0:T(8,128)S(1)} collective-permute-done((f32[64,128]{1,0:T(8,128)S(1)}, f32[64,128]{1,0:T(8,128)S(1)}, u32[]{:S(2)}, u32[]{:S(2)}) %collective-permute-start.1) | collective-permute-done | bytes 32800 | tf_op jit(solution)/shard_map/ppermute | solution.py:249
  9.0 0.1 shard_map.48
  9.1 2.7 %collective-permute-start.4 = (f32[8,128]{1,0:T(8,128)S(1)}, f32[8,128]{1,0:T(8,128)S(1)}, u32[]{:S(2)}, u32[]{:S(2)}) collective-permute-start(f32[8,128]{1,0:T(8,128)S(1)} %get-tuple-element.25), channel_id=1, source_target_pairs={{0,4},{1,5},{2,6},{3,7},{4,0},{5,1},{6,2},{7,3},{8,12},{9,13},{10,... | collective-permute-start | bytes 12296 | tf_op jit(solution)/shard_map/ppermute | solution.py:261
  11.8 0.0 collective-permute-start.5
  11.8 0.0 copy-done
  11.8 2.3 %shard_map.49 = (f32[4096,128]{1,0:T(8,128)S(1)}, bf16[4,64,64]{2,1,0:T(8,128)(2,1)S(1)}, bf16[4,64,64]{2,1,0:T(8,128)(2,1)S(1)}) custom-call(f32[4096,128]{1,0:T(8,128)S(1)} %get-tuple-element.16.cot, f32[4,64,64]{2,1,0:T(8,128)S(1)} %copy-done, f32[16,128]{1,0:T(8,128)S(1)} %get-tuple-element.17.kappa, f32[64,128]{1,0:T(8,128)S(1)} %get-tuple-element.19.spread), custom_call_target="tpu_custom_call" | custom-call | flops 201326592 | bytes 4194304 | tf_op jit(solution)/shard_map/pallas_call | solution.py:16
  14.1 0.0 collective-permute-done.4.near_c
  14.1 2.1 %collective-permute-done.5.far_c = f32[8,128]{1,0:T(8,128)S(1)} collective-permute-done((f32[8,128]{1,0:T(8,128)S(1)}, f32[8,128]{1,0:T(8,128)S(1)}, u32[]{:S(2)}, u32[]{:S(2)}) %collective-permute-start.5) | collective-permute-done | bytes 4128 | tf_op jit(solution)/shard_map/ppermute | solution.py:260
  16.3 0.0 collective-permute-done.2.near
  16.3 0.0 collective-permute-done.3.far
  16.3 1.6 %shard_map.50 = f32[4096,128]{1,0:T(8,128)} custom-call(f32[4096,128]{1,0:T(8,128)S(1)} %get-tuple-element.20.base_out, bf16[4,64,64]{2,1,0:T(8,128)(2,1)S(1)} %get-tuple-element.21.high, bf16[4,64,64]{2,1,0:T(8,128)(2,1)S(1)} %get-tuple-element.22.low, f32[256,128]{1,0:T(8,128)S(1)} %collective-permute-done.2.near, ...), custom_call_target="tpu_custom_call" | custom-call | flops 2097152 | bytes 4194304 | tf_op jit(solution)/shard_map/pallas_call | solution.py:16
  (1 shorter events, 0.0 us)
Async XLA Ops:
  0.0 11.8 %copy-start = (f32[4,64,64]{2,1,0:T(8,128)S(1)}, f32[4,64,64]{2,1,0:T(8,128)}, u32[]{:S(2)}) copy-start(f32[4,64,64]{2,1,0:T(8,128)} %blocks.1) | copy-start | bytes 196612
  1.7 14.5 %collective-permute-start.2 = (f32[256,128]{1,0:T(8,128)S(1)}, f32[256,128]{1,0:T(8,128)S(1)}, u32[]{:S(2)}, u32[]{:S(2)}) collective-permute-start(f32[256,128]{1,0:T(8,128)S(1)} %get-tuple-element.23), channel_id=1, source_target_pairs={{0,4},{1,5},{2,6},{3,7},{4,0},{5,1},{6,2},{7,3},{8,12},{9,13},{10,... | collective-permute-start | bytes 393224 | tf_op jit(solution)/shard_map/ppermute | solution.py:242
  3.3 13.0 %collective-permute-start.3 = (f32[256,128]{1,0:T(8,128)S(1)}, f32[256,128]{1,0:T(8,128)S(1)}, u32[]{:S(2)}, u32[]{:S(2)}) collective-permute-start(f32[256,128]{1,0:T(8,128)S(1)} %get-tuple-element.24), channel_id=1, source_target_pairs={{0,1},{1,0},{2,3},{3,2},{4,8},{5,9},{6,10},{7,11},{8,4},{9,5},{10,... | collective-permute-start | bytes 393224 | tf_op jit(solution)/shard_map/ppermute | solution.py:250
  3.7 1.3 %collective-permute-start = (f32[128,128]{1,0:T(8,128)S(1)}, f32[128,128]{1,0:T(8,128)S(1)}, u32[]{:S(2)}, u32[]{:S(2)}) collective-permute-start(f32[128,128]{1,0:T(8,128)S(1)} %get-tuple-element.18.own), channel_id=1, source_target_pairs={{0,1},{1,0},{2,3},{3,2},{4,5},{5,4},{6,7},{7,6},{8,9},{9,8},{10,11... | collective-permute-start | bytes 196616 | tf_op jit(solution)/shard_map/ppermute | solution.py:241
  5.0 4.0 %collective-permute-start.1 = (f32[64,128]{1,0:T(8,128)S(1)}, f32[64,128]{1,0:T(8,128)S(1)}, u32[]{:S(2)}, u32[]{:S(2)}) collective-permute-start(f32[64,128]{1,0:T(8,128)S(1)} %shard_map.47), channel_id=1, source_target_pairs={{2,0},{3,1},{0,2},{1,3},{6,4},{7,5},{4,6},{5,7},{10,8},{11,9},{8,1... | collective-permute-start | bytes 98312 | tf_op jit(solution)/shard_map/ppermute | solution.py:249
  9.1 5.0 %collective-permute-start.4 = (f32[8,128]{1,0:T(8,128)S(1)}, f32[8,128]{1,0:T(8,128)S(1)}, u32[]{:S(2)}, u32[]{:S(2)}) collective-permute-start(f32[8,128]{1,0:T(8,128)S(1)} %get-tuple-element.25), channel_id=1, source_target_pairs={{0,4},{1,5},{2,6},{3,7},{4,0},{5,1},{6,2},{7,3},{8,12},{9,13},{10,... | collective-permute-start | bytes 12296 | tf_op jit(solution)/shard_map/ppermute | solution.py:261
  11.8 4.5 %collective-permute-start.5 = (f32[8,128]{1,0:T(8,128)S(1)}, f32[8,128]{1,0:T(8,128)S(1)}, u32[]{:S(2)}, u32[]{:S(2)}) collective-permute-start(f32[8,128]{1,0:T(8,128)S(1)} %get-tuple-element.26), channel_id=1, source_target_pairs={{0,1},{1,0},{2,3},{3,2},{4,8},{5,9},{6,10},{7,11},{8,4},{9,5},{10,... | collective-permute-start | bytes 12296 | tf_op jit(solution)/shard_map/ppermute | solution.py:260

commit v3 on v2

--- a/solution.py
+++ b/solution.py
@@ -34,10 +34,10 @@
     return high, low
 
 
-def product(high, low, x):
-    a, b = halves(x)
-    dot = functools.partial(jnp.dot, preferred_element_type=jnp.float32)
-    return dot(high, a) + (dot(high, b) + dot(low, a))
+def product(matrix, x):
+    high, low = halves(x)
+    stacked = jnp.concatenate([high, low, high], axis=0)
+    return jnp.dot(matrix, stacked, preferred_element_type=jnp.float32)
 
 
 def even_strip():
@@ -134,32 +134,38 @@
         second[f : f + 1, :] = jnp.where(even, low, high)
 
 
-def main_kernel(dims, cot, blocks, kappa, spread, out, high_ref, low_ref):
+def main_kernel(dims, cot, blocks, kappa, spread, out, matrices):
     fields, levels, rows = dims
-    top = lax.broadcasted_iota(jnp.int32, (levels, kappa.shape[1]), 0) == levels - 1
+    columns = kappa.shape[1]
+    top = lax.broadcasted_iota(jnp.int32, (levels, columns), 0) == levels - 1
     for f in range(fields):
         high, low = halves(jnp.transpose(blocks[f]))
-        high_ref[f], low_ref[f] = high, low
+        matrix = jnp.concatenate([high, high, low], axis=1)
+        matrices[f] = matrix
         base = f * levels * rows
-        load = lambda x: cot[pl.ds(base + x, levels, stride=rows), :]
-        scaled = lambda x, v: v * kappa[x : x + 1, :]
-        before = None
-        here = load(0)
-        here_w = scaled(0, here)
+        at = lambda x: pl.ds(base + x, levels, stride=rows)
+        before, here = None, cot[at(0), :]
+        here_w = here * kappa[0:1, :]
+        totals = []
         for x in range(rows):
             total = here - 4.0 * here_w + across(here_w)
             if before is not None:
                 total = total + before
+            before = here_w
             if x + 1 < rows:
-                after = load(x + 1)
-                after_w = scaled(x + 1, after)
-                total = total + after_w
-            total = total + jnp.where(top, spread[f * rows + x : f * rows + x + 1, :], 0.0)
-            out[pl.ds(base + x, levels, stride=rows), :] = product(high, low, total)
-            before, here, here_w = here_w, after, after_w
-
-
-def final_kernel(dims, strips, base_out, high, low, near, far, near_c, far_c, out_hbm, out, sems):
+                here = cot[at(x + 1), :]
+                here_w = here * kappa[x + 1 : x + 2, :]
+                total = total + here_w
+            totals.append(total + jnp.where(top, spread[f * rows + x : f * rows + x + 1, :], 0.0))
+            if len(totals) == 2 or x + 1 == rows:
+                result = product(matrix, jnp.concatenate(totals, axis=1))
+                for i in range(len(totals)):
+                    start = x + 1 - len(totals) + i
+                    out[at(start), :] = result[:, i * columns : (i + 1) * columns]
+                totals = []
+
+
+def final_kernel(dims, strips, base_out, matrices, near, far, near_c, far_c, out_hbm, out, sems):
     fields, levels, rows = dims
     chunk = levels * rows
     columns = near.shape[1]
@@ -179,7 +185,7 @@
             sides.append(jnp.where(here, value, 0.0))
         below = jnp.where(even, sides[1], sides[0])
         above = jnp.where(even, sides[0], sides[1])
-        extra = product(high[f], low[f], jnp.concatenate([below, above], axis=1))
+        extra = product(matrices[f], jnp.concatenate([below, above], axis=1))
         for x, part in ((0, extra[:, :columns]), (rows - 1, extra[:, columns:])):
             at = pl.ds(base + x, levels, stride=rows)
             out[at, :] = out[at, :] + part
@@ -222,7 +228,7 @@
     size = fields * rows
     edge = f32(fields * levels, columns)
     nbytes = 4 * cot.size
-    square = jax.ShapeDtypeStruct((fields, levels, levels), jnp.bfloat16)
+    wide = jax.ShapeDtypeStruct((fields, levels, 3 * levels), jnp.bfloat16)
     tiny = f32(-(-fields // 8) * 8, columns)
     whole = ("strip", "lev")
     one, two = swaps(strips, pieces, 0), swaps(strips, pieces, 1)
@@ -259,9 +265,9 @@
     )
     far_c = lax.ppermute(second, whole, two)
     near_c = lax.ppermute(first, whole, one)
-    base_out, high, low = call(
+    base_out, matrices = call(
         functools.partial(main_kernel, dims),
-        [f32(*cot.shape), square, square],
+        [f32(*cot.shape), wide],
         (6 * levels * cot.size, 2 * nbytes),
         cot,
         blocks,
@@ -273,8 +279,7 @@
         [f32(*cot.shape)],
         (4 * cot.size, 2 * nbytes),
         base_out,
-        high,
-        low,
+        matrices,
         near,
         far,
         near_c,

time: 18 us -> 18 us (level)
  Pallas kernels: 5.77 us -> 5.56 us
    pallas_call x5, Pallas kernels: 5.77 us -> 5.56 us  [call(): pl.pallas_call(body, out_shape=outs, in_specs=ins or [VMEM] * len(args),...]
  transfers between devices with their start and end apart: 6 -> 6, of which waited for: 3 -> 3; matrix products, arithmetic and copies ran while one was open for 0% -> 0% of each run, Pallas kernels for 14% -> 13%
where the time goes in v3:
time: 18 us; the launch traced here: 17.8 us
  waiting for transfers between devices  7.39 us (41%)
  Pallas kernels  5.56 us (31%)
  starting transfers between devices  4.82 us (27%)
    pallas_call x5, Pallas kernels, call(): pl.pallas_call(body, out_shape=outs, in_specs=ins or [VMEM] * len(args),...  5.56 us
    ppermute x1, waiting for transfers between devices, compute(): received.append(lax.ppermute(chip, 'lev', moves))  3.83 us
    ppermute x1, starting transfers between devices, compute(): near_c = lax.ppermute(first, whole, one)  2.68 us
    ppermute x1, waiting for transfers between devices, compute(): far_c = lax.ppermute(second, whole, two)  2.31 us
    ppermute x1, starting transfers between devices, compute(): near = lax.ppermute(first, whole, one)  1.56 us
    ppermute x1, waiting for transfers between devices, compute(): other = lax.ppermute(pair, 'lev', [(i, i ^ 1) for i in range(pieces)])  1.25 us
    ppermute x1, starting transfers between devices, compute(): far = lax.ppermute(second, whole, two)  0.42 us
  transfers between devices with their start and end apart: 6, of which 3 were waited for; matrix products, arithmetic and copies ran while one was open for 0% of the time, Pallas kernels for 13%

profile of v3, /device:TPU:12, one launch (start us, length us, event | category | flops | bytes accessed | tf_op | source)
XLA Modules:
  0.0 17.8 jit_solution(11896991482161555813)
XLA Ops:
  0.0 0.0 copy-start
  0.0 1.7 %shard_map.46 = (f32[4096,128]{1,0:T(8,128)S(1)}, f32[16,128]{1,0:T(8,128)S(1)}, f32[256,128]{1,0:T(8,128)S(1)}, f32[256,128]{1,0:T(8,128)S(1)}, f32[128,128]{1,0:T(8,128)S(1)}) custom-call(f32[4096,128]{1,0:T(8,128)} %bitcast.3, f32[64,128]{1,0:T(8,128)} %bitcast.4, f32[16,128]{1,0:T(8,128)} %kappa_hbm.1), custom_call_target="tpu_custom_call" | custom-call | flops 524288 | bytes 2097152 | tf_op jit(solution)/shard_map/pallas_call | solution.py:16
  1.7 1.6 %collective-permute-start.2 = (f32[256,128]{1,0:T(8,128)S(1)}, f32[256,128]{1,0:T(8,128)S(1)}, u32[]{:S(2)}, u32[]{:S(2)}) collective-permute-start(f32[256,128]{1,0:T(8,128)S(1)} %get-tuple-element.21), channel_id=1, source_target_pairs={{0,4},{1,5},{2,6},{3,7},{4,0},{5,1},{6,2},{7,3},{8,12},{9,13},{10,... | collective-permute-start | bytes 393224 | tf_op jit(solution)/shard_map/ppermute | solution.py:248
  3.3 0.4 %collective-permute-start.3 = (f32[256,128]{1,0:T(8,128)S(1)}, f32[256,128]{1,0:T(8,128)S(1)}, u32[]{:S(2)}, u32[]{:S(2)}) collective-permute-start(f32[256,128]{1,0:T(8,128)S(1)} %get-tuple-element.22), channel_id=1, source_target_pairs={{0,1},{1,0},{2,3},{3,2},{4,8},{5,9},{6,10},{7,11},{8,4},{9,5},{10,... | collective-permute-start | bytes 393224 | tf_op jit(solution)/shard_map/ppermute | solution.py:256
  3.7 0.0 collective-permute-start
  3.7 1.3 %collective-permute-done.other = f32[128,128]{1,0:T(8,128)S(1)} collective-permute-done((f32[128,128]{1,0:T(8,128)S(1)}, f32[128,128]{1,0:T(8,128)S(1)}, u32[]{:S(2)}, u32[]{:S(2)}) %collective-permute-start) | collective-permute-done | bytes 65568 | tf_op jit(solution)/shard_map/ppermute | solution.py:247
  5.0 0.2 collective-permute-start.1
  5.1 3.8 %collective-permute-done.1.refs_0_ = f32[64,128]{1,0:T(8,128)S(1)} collective-permute-done((f32[64,128]{1,0:T(8,128)S(1)}, f32[64,128]{1,0:T(8,128)S(1)}, u32[]{:S(2)}, u32[]{:S(2)}) %collective-permute-start.1) | collective-permute-done | bytes 32800 | tf_op jit(solution)/shard_map/ppermute | solution.py:255
  9.0 0.1 shard_map.48
  9.1 2.7 %collective-permute-start.4 = (f32[8,128]{1,0:T(8,128)S(1)}, f32[8,128]{1,0:T(8,128)S(1)}, u32[]{:S(2)}, u32[]{:S(2)}) collective-permute-start(f32[8,128]{1,0:T(8,128)S(1)} %get-tuple-element.23), channel_id=1, source_target_pairs={{0,4},{1,5},{2,6},{3,7},{4,0},{5,1},{6,2},{7,3},{8,12},{9,13},{10,... | collective-permute-start | bytes 12296 | tf_op jit(solution)/shard_map/ppermute | solution.py:267
  11.8 0.0 collective-permute-start.5
  11.8 0.0 copy-done
  11.8 2.2 %shard_map.49 = (f32[4096,128]{1,0:T(8,128)S(1)}, bf16[4,64,192]{2,1,0:T(8,128)(2,1)S(1)}) custom-call(f32[4096,128]{1,0:T(8,128)S(1)} %get-tuple-element.15.cot, f32[4,64,64]{2,1,0:T(8,128)S(1)} %copy-done, f32[16,128]{1,0:T(8,128)S(1)} %get-tuple-element.16.kappa, f32[64,128]{1,0:T(8,128)S(1)} %get-tuple-element.18.spread), custom_call_target="tpu_custom_call" | custom-call | flops 201326592 | bytes 4194304 | tf_op jit(solution)/shard_map/pallas_call | solution.py:16
  13.9 0.0 collective-permute-done.4.near_c
  14.0 2.3 %collective-permute-done.5.far_c = f32[8,128]{1,0:T(8,128)S(1)} collective-permute-done((f32[8,128]{1,0:T(8,128)S(1)}, f32[8,128]{1,0:T(8,128)S(1)}, u32[]{:S(2)}, u32[]{:S(2)}) %collective-permute-start.5) | collective-permute-done | bytes 4128 | tf_op jit(solution)/shard_map/ppermute | solution.py:266
  16.3 0.0 collective-permute-done.2.near
  16.3 0.0 collective-permute-done.3.far
  16.3 1.5 %shard_map.50 = f32[4096,128]{1,0:T(8,128)} custom-call(f32[4096,128]{1,0:T(8,128)S(1)} %get-tuple-element.19.base_out, bf16[4,64,192]{2,1,0:T(8,128)(2,1)S(1)} %get-tuple-element.20.matrices, f32[256,128]{1,0:T(8,128)S(1)} %collective-permute-done.2.near, f32[256,128]{1,0:T(8,128)S(1)} %collective-permute-done.3.far, ...), custom_call_target="tpu_custom_call" | custom-call | flops 2097152 | bytes 4194304 | tf_op jit(solution)/shard_map/pallas_call | solution.py:16
  (1 shorter events, 0.0 us)
Async XLA Ops:
  0.0 11.8 %copy-start = (f32[4,64,64]{2,1,0:T(8,128)S(1)}, f32[4,64,64]{2,1,0:T(8,128)}, u32[]{:S(2)}) copy-start(f32[4,64,64]{2,1,0:T(8,128)} %blocks.1) | copy-start | bytes 196612
  1.7 14.5 %collective-permute-start.2 = (f32[256,128]{1,0:T(8,128)S(1)}, f32[256,128]{1,0:T(8,128)S(1)}, u32[]{:S(2)}, u32[]{:S(2)}) collective-permute-start(f32[256,128]{1,0:T(8,128)S(1)} %get-tuple-element.21), channel_id=1, source_target_pairs={{0,4},{1,5},{2,6},{3,7},{4,0},{5,1},{6,2},{7,3},{8,12},{9,13},{10,... | collective-permute-start | bytes 393224 | tf_op jit(solution)/shard_map/ppermute | solution.py:248
  3.3 13.0 %collective-permute-start.3 = (f32[256,128]{1,0:T(8,128)S(1)}, f32[256,128]{1,0:T(8,128)S(1)}, u32[]{:S(2)}, u32[]{:S(2)}) collective-permute-start(f32[256,128]{1,0:T(8,128)S(1)} %get-tuple-element.22), channel_id=1, source_target_pairs={{0,1},{1,0},{2,3},{3,2},{4,8},{5,9},{6,10},{7,11},{8,4},{9,5},{10,... | collective-permute-start | bytes 393224 | tf_op jit(solution)/shard_map/ppermute | solution.py:256
  3.7 1.3 %collective-permute-start = (f32[128,128]{1,0:T(8,128)S(1)}, f32[128,128]{1,0:T(8,128)S(1)}, u32[]{:S(2)}, u32[]{:S(2)}) collective-permute-start(f32[128,128]{1,0:T(8,128)S(1)} %get-tuple-element.17.own), channel_id=1, source_target_pairs={{0,1},{1,0},{2,3},{3,2},{4,5},{5,4},{6,7},{7,6},{8,9},{9,8},{10,11... | collective-permute-start | bytes 196616 | tf_op jit(solution)/shard_map/ppermute | solution.py:247
  5.0 4.0 %collective-permute-start.1 = (f32[64,128]{1,0:T(8,128)S(1)}, f32[64,128]{1,0:T(8,128)S(1)}, u32[]{:S(2)}, u32[]{:S(2)}) collective-permute-start(f32[64,128]{1,0:T(8,128)S(1)} %shard_map.47), channel_id=1, source_target_pairs={{2,0},{3,1},{0,2},{1,3},{6,4},{7,5},{4,6},{5,7},{10,8},{11,9},{8,1... | collective-permute-start | bytes 98312 | tf_op jit(solution)/shard_map/ppermute | solution.py:255
  9.1 4.9 %collective-permute-start.4 = (f32[8,128]{1,0:T(8,128)S(1)}, f32[8,128]{1,0:T(8,128)S(1)}, u32[]{:S(2)}, u32[]{:S(2)}) collective-permute-start(f32[8,128]{1,0:T(8,128)S(1)} %get-tuple-element.23), channel_id=1, source_target_pairs={{0,4},{1,5},{2,6},{3,7},{4,0},{5,1},{6,2},{7,3},{8,12},{9,13},{10,... | collective-permute-start | bytes 12296 | tf_op jit(solution)/shard_map/ppermute | solution.py:267
  11.8 4.5 %collective-permute-start.5 = (f32[8,128]{1,0:T(8,128)S(1)}, f32[8,128]{1,0:T(8,128)S(1)}, u32[]{:S(2)}, u32[]{:S(2)}) collective-permute-start(f32[8,128]{1,0:T(8,128)S(1)} %get-tuple-element.24), channel_id=1, source_target_pairs={{0,1},{1,0},{2,3},{3,2},{4,8},{5,9},{6,10},{7,11},{8,4},{9,5},{10,... | collective-permute-start | bytes 12296 | tf_op jit(solution)/shard_map/ppermute | solution.py:266

commit v4 on v3

--- a/solution.py
+++ b/solution.py
@@ -10,15 +10,17 @@
 VMEM = pl.BlockSpec(memory_space=pltpu.VMEM)
 HBM = pl.BlockSpec(memory_space=pltpu.HBM)
 LIMIT = 16 * 1024 * 1024
-
-
-def call(body, outs, cost, *args, ins=None, out_specs=None, scratch=()):
+LATE = 1
+
+
+def call(body, outs, cost, *args, ins=None, out_specs=None, scratch=(), aliases=None):
     return pl.pallas_call(
         body,
         out_shape=outs,
         in_specs=ins or [VMEM] * len(args),
         out_specs=out_specs or [VMEM] * len(outs),
         scratch_shapes=list(scratch),
+        input_output_aliases=aliases or {},
         compiler_params=pltpu.CompilerParams(vmem_limit_bytes=LIMIT),
         cost_estimate=pl.CostEstimate(flops=cost[0], bytes_accessed=cost[1], transcendentals=0),
     )(*args)
@@ -40,7 +42,7 @@
     return jnp.dot(matrix, stacked, preferred_element_type=jnp.float32)
 
 
-def even_strip():
+def first_is_above():
     return lax.rem(lax.axis_index("strip"), 2) == 0
 
 
@@ -63,18 +65,19 @@
         copy.start()
     for copy in small:
         copy.wait()
-    even = even_strip()
+    size = fields * rows
+    pair[size:, :] = couple[...]
+    is_above = first_is_above()
     for f in range(fields):
         large[f].wait()
         base = f * chunk
         low = kappa[0:1, :] * cot[pl.ds(base, levels, stride=rows), :]
         high = kappa[rows - 1 : rows, :] * cot[pl.ds(base + rows - 1, levels, stride=rows), :]
-        first[f * levels : (f + 1) * levels, :] = jnp.where(even, high, low)
-        second[f * levels : (f + 1) * levels, :] = jnp.where(even, low, high)
+        first[f * levels : (f + 1) * levels, :] = jnp.where(is_above, high, low)
+        second[f * levels : (f + 1) * levels, :] = jnp.where(is_above, low, high)
+        mine = slice(f * rows, (f + 1) * rows)
         block = cot[base : base + chunk, :].reshape(levels, rows, -1)
-        weight = couple[f * rows : (f + 1) * rows, :]
-        pair[f * rows : (f + 1) * rows, :] = weight * jnp.sum(block, axis=0)
-        pair[(fields + f) * rows : (fields + f + 1) * rows, :] = weight
+        pair[mine, :] = couple[mine, :] * jnp.sum(block, axis=0)
 
 
 def chip_pair(mine, own, other, size):
@@ -126,71 +129,92 @@
     spread[...] = carried - 4.0 * weighted + across(weighted) + below + above
     first[...] = jnp.zeros_like(first)
     second[...] = jnp.zeros_like(second)
-    even = even_strip()
+    is_above = first_is_above()
     for f in range(fields):
         low = weighted[f * rows : f * rows + 1, :]
         high = weighted[(f + 1) * rows - 1 : (f + 1) * rows, :]
-        first[f : f + 1, :] = jnp.where(even, high, low)
-        second[f : f + 1, :] = jnp.where(even, low, high)
-
-
-def main_kernel(dims, cot, blocks, kappa, spread, out, matrices):
+        first[f : f + 1, :] = jnp.where(is_above, high, low)
+        second[f : f + 1, :] = jnp.where(is_above, low, high)
+
+
+def writes(dims, stage, out, sems, late):
+    fields, levels, rows = dims
+    split = (fields - LATE) * levels
+    part = pl.ds(split, LATE * levels) if late else pl.ds(0, split)
+    return [
+        pltpu.make_async_copy(stage.at[x, part], out.at[part, x, 0], sems.at[x])
+        for x in range(1, rows - 1)
+        if LATE or not late
+    ]
+
+
+def main_kernel(dims, cot, blocks, kappa, spread, out, stage, matrices, sems):
     fields, levels, rows = dims
     columns = kappa.shape[1]
-    top = lax.broadcasted_iota(jnp.int32, (levels, columns), 0) == levels - 1
+    top = lax.broadcasted_iota(jnp.int32, (8, columns), 0) == 7
+    copies = writes(dims, stage, out, sems, False)
     for f in range(fields):
         high, low = halves(jnp.transpose(blocks[f]))
         matrix = jnp.concatenate([high, high, low], axis=1)
         matrices[f] = matrix
-        base = f * levels * rows
-        at = lambda x: pl.ds(base + x, levels, stride=rows)
-        before, here = None, cot[at(0), :]
+        load = lambda x: cot[pl.ds(f * levels * rows + x, levels, stride=rows), :]
+        before, here = None, load(0)
         here_w = here * kappa[0:1, :]
         totals = []
         for x in range(rows):
-            total = here - 4.0 * here_w + across(here_w)
+            total = here * (1.0 - 4.0 * kappa[x : x + 1, :]) + across(here_w)
             if before is not None:
                 total = total + before
             before = here_w
             if x + 1 < rows:
-                here = cot[at(x + 1), :]
+                here = load(x + 1)
                 here_w = here * kappa[x + 1 : x + 2, :]
                 total = total + here_w
-            totals.append(total + jnp.where(top, spread[f * rows + x : f * rows + x + 1, :], 0.0))
-            if len(totals) == 2 or x + 1 == rows:
-                result = product(matrix, jnp.concatenate(totals, axis=1))
-                for i in range(len(totals)):
-                    start = x + 1 - len(totals) + i
-                    out[at(start), :] = result[:, i * columns : (i + 1) * columns]
-                totals = []
-
-
-def final_kernel(dims, strips, base_out, matrices, near, far, near_c, far_c, out_hbm, out, sems):
+            carry = jnp.where(top, spread[f * rows + x : f * rows + x + 1, :], 0.0)
+            total = jnp.concatenate([total[: levels - 8], total[levels - 8 :] + carry], axis=0)
+            totals.append(total)
+            if len(totals) < 2 and x + 1 < rows:
+                continue
+            result = product(matrix, jnp.concatenate(totals, axis=1))
+            for i in range(len(totals)):
+                row = x + 1 - len(totals) + i
+                stage[row, f * levels : (f + 1) * levels] = result[:, i * columns : (i + 1) * columns]
+            totals = []
+        if f + 1 == fields - LATE:
+            for copy in copies:
+                copy.start()
+    for copy in copies:
+        copy.wait()
+
+
+def final_kernel(
+    dims, strips, started, stage, matrices, first, second, first_c, second_c, out, edges, sems
+):
     fields, levels, rows = dims
-    chunk = levels * rows
-    columns = near.shape[1]
+    columns = first.shape[1]
+    copies = writes(dims, stage, out, sems, True)
+    for copy in copies:
+        copy.start()
     mine = lax.axis_index("strip")
-    even = even_strip()
-    has_near = jnp.logical_or(jnp.logical_not(even), mine + 1 < strips)
-    has_far = jnp.where(even, mine > 0, mine + 1 < strips)
-    top = lax.broadcasted_iota(jnp.int32, (levels, columns), 0) == levels - 1
-    copies = []
+    is_above = first_is_above()
+    below_exists, above_exists = mine > 0, mine + 1 < strips
+    top = lax.broadcasted_iota(jnp.int32, (8, columns), 0) == 7
     for f in range(fields):
-        base = f * chunk
-        out[base : base + chunk, :] = base_out[base : base + chunk, :]
+        at = slice(f * levels, (f + 1) * levels)
         sides = []
-        for here, halo, halo_c in ((has_near, near, near_c), (has_far, far, far_c)):
-            value = halo[f * levels : (f + 1) * levels, :]
-            value = value + jnp.where(top, halo_c[f : f + 1, :], 0.0)
-            sides.append(jnp.where(here, value, 0.0))
-        below = jnp.where(even, sides[1], sides[0])
-        above = jnp.where(even, sides[0], sides[1])
+        for halo, halo_c in ((first, first_c), (second, second_c)):
+            carry = jnp.where(top, halo_c[f : f + 1, :], 0.0)
+            value = halo[at, :]
+            sides.append(
+                jnp.concatenate([value[: levels - 8], value[levels - 8 :] + carry], axis=0)
+            )
+        below = jnp.where(below_exists, jnp.where(is_above, sides[1], sides[0]), 0.0)
+        above = jnp.where(above_exists, jnp.where(is_above, sides[0], sides[1]), 0.0)
         extra = product(matrices[f], jnp.concatenate([below, above], axis=1))
-        for x, part in ((0, extra[:, :columns]), (rows - 1, extra[:, columns:])):
-            at = pl.ds(base + x, levels, stride=rows)
-            out[at, :] = out[at, :] + part
-        span = pl.ds(base, chunk)
-        copies.append(pltpu.make_async_copy(out.at[span], out_hbm.at[span], sems.at[f]))
+        for side, x in ((0, 0), (1, rows - 1)):
+            edges[side, at] = stage[x, at] + extra[:, side * columns : (side + 1) * columns]
+    for side, x in ((0, 0), (1, rows - 1)):
+        copies.append(pltpu.make_async_copy(edges.at[side], out.at[:, x, 0], sems.at[x]))
         copies[-1].start()
     for copy in copies:
         copy.wait()
@@ -208,10 +232,10 @@
     return [(i + step) % count for i in range(count)]
 
 
-def swaps(strips, pieces, shift):
+def swaps(strips, pieces, turn):
     pairs = []
     for strip in range(strips):
-        other = ((strip + shift) ^ 1) - shift
+        other = ((strip + turn) ^ 1) - turn
         for piece in range(pieces):
             mine = strip * pieces + piece
             inside = 0 <= other < strips
@@ -225,6 +249,8 @@
     chips = pieces // 2
     dims = (fields, levels, rows)
     cot = cotangent.reshape(fields * levels * rows, columns)
+    rowwise = f32(fields * levels, rows, 1, columns)
+    by_row = f32(rows, fields * levels, columns)
     size = fields * rows
     edge = f32(fields * levels, columns)
     nbytes = 4 * cot.size
@@ -233,7 +259,7 @@
     whole = ("strip", "lev")
     one, two = swaps(strips, pieces, 0), swaps(strips, pieces, 1)
 
-    cot, kappa, first, second, pair = call(
+    held, kappa, first, second, pair = call(
         functools.partial(pack_kernel, dims),
         [f32(*cot.shape), f32(rows, columns), edge, edge, f32(2 * size, columns)],
         (cot.size, nbytes),
@@ -265,27 +291,35 @@
     )
     far_c = lax.ppermute(second, whole, two)
     near_c = lax.ppermute(first, whole, one)
-    base_out, matrices = call(
+    started, stage, matrices = call(
         functools.partial(main_kernel, dims),
-        [f32(*cot.shape), wide],
+        [rowwise, by_row, wide],
         (6 * levels * cot.size, 2 * nbytes),
-        cot,
+        held,
         blocks,
         kappa,
         spread,
+        out_specs=[HBM, VMEM, VMEM],
+        scratch=[pltpu.SemaphoreType.DMA((rows,))],
     )
     (out,) = call(
         functools.partial(final_kernel, dims, strips),
-        [f32(*cot.shape)],
-        (4 * cot.size, 2 * nbytes),
-        base_out,
+        [rowwise],
+        (cot.size, nbytes // 4),
+        started,
+        stage,
         matrices,
         near,
         far,
         near_c,
         far_c,
+        ins=[HBM] + [VMEM] * 6,
         out_specs=[HBM],
-        scratch=[pltpu.VMEM(cot.shape, jnp.float32), pltpu.SemaphoreType.DMA((fields,))],
+        scratch=[
+            pltpu.VMEM((2, fields * levels, columns), jnp.float32),
+            pltpu.SemaphoreType.DMA((rows,)),
+        ],
+        aliases={0: 0},
     )
     return out.reshape(cotangent.shape)
 

time: 18 us -> 17.5 us (0.972)
  waiting for transfers between devices: 7.39 us -> 7 us
    ppermute x1, waiting for transfers between devices: 2.31 us -> 1.92 us  [compute(): far_c = lax.ppermute(second, whole, two)]
  transfers between devices with their start and end apart: 6 -> 6, of which waited for: 3 -> 3; matrix products, arithmetic and copies ran while one was open for 0% -> 0% of each run, Pallas kernels for 13% -> 15%
where the time goes in v4:
time: 17.5 us; the launch traced here: 17.3 us
  waiting for transfers between devices  7 us (40%)
  Pallas kernels  5.47 us (31%)
  starting transfers between devices  4.82 us (28%)
    pallas_call x5, Pallas kernels, call(): pl.pallas_call(body, out_shape=outs, in_specs=ins or [VMEM] * len(args),...  5.47 us
    ppermute x1, waiting for transfers between devices, compute(): received.append(lax.ppermute(chip, 'lev', moves))  3.83 us
    ppermute x1, starting transfers between devices, compute(): near_c = lax.ppermute(first, whole, one)  2.68 us
    ppermute x1, waiting for transfers between devices, compute(): far_c = lax.ppermute(second, whole, two)  1.92 us
    ppermute x1, starting transfers between devices, compute(): near = lax.ppermute(first, whole, one)  1.56 us
    ppermute x1, waiting for transfers between devices, compute(): other = lax.ppermute(pair, 'lev', [(i, i ^ 1) for i in range(pieces)])  1.25 us
    ppermute x1, starting transfers between devices, compute(): far = lax.ppermute(second, whole, two)  0.42 us
  transfers between devices with their start and end apart: 6, of which 3 were waited for; matrix products, arithmetic and copies ran while one was open for 0% of the time, Pallas kernels for 15%

profile of v4, /device:TPU:12, one launch (start us, length us, event | category | flops | bytes accessed | tf_op | source)
XLA Modules:
  0.0 17.3 jit_solution(13357126084357610419)
XLA Ops:
  0.0 0.0 copy-start
  0.0 1.7 %shard_map.46 = (f32[4096,128]{1,0:T(8,128)S(1)}, f32[16,128]{1,0:T(8,128)S(1)}, f32[256,128]{1,0:T(8,128)S(1)}, f32[256,128]{1,0:T(8,128)S(1)}, f32[128,128]{1,0:T(8,128)S(1)}) custom-call(f32[4096,128]{1,0:T(8,128)} %bitcast.3, f32[64,128]{1,0:T(8,128)} %bitcast.4, f32[16,128]{1,0:T(8,128)} %kappa_hbm.1), custom_call_target="tpu_custom_call" | custom-call | flops 524288 | bytes 2097152 | tf_op jit(solution)/shard_map/pallas_call | solution.py:17
  1.7 1.6 %collective-permute-start.2 = (f32[256,128]{1,0:T(8,128)S(1)}, f32[256,128]{1,0:T(8,128)S(1)}, u32[]{:S(2)}, u32[]{:S(2)}) collective-permute-start(f32[256,128]{1,0:T(8,128)S(1)} %get-tuple-element.23), channel_id=1, source_target_pairs={{0,4},{1,5},{2,6},{3,7},{4,0},{5,1},{6,2},{7,3},{8,12},{9,13},{10,... | collective-permute-start | bytes 393224 | tf_op jit(solution)/shard_map/ppermute | solution.py:274
  3.3 0.4 %collective-permute-start.3 = (f32[256,128]{1,0:T(8,128)S(1)}, f32[256,128]{1,0:T(8,128)S(1)}, u32[]{:S(2)}, u32[]{:S(2)}) collective-permute-start(f32[256,128]{1,0:T(8,128)S(1)} %get-tuple-element.24), channel_id=1, source_target_pairs={{0,1},{1,0},{2,3},{3,2},{4,8},{5,9},{6,10},{7,11},{8,4},{9,5},{10,... | collective-permute-start | bytes 393224 | tf_op jit(solution)/shard_map/ppermute | solution.py:282
  3.7 0.0 collective-permute-start
  3.7 1.3 %collective-permute-done.other = f32[128,128]{1,0:T(8,128)S(1)} collective-permute-done((f32[128,128]{1,0:T(8,128)S(1)}, f32[128,128]{1,0:T(8,128)S(1)}, u32[]{:S(2)}, u32[]{:S(2)}) %collective-permute-start) | collective-permute-done | bytes 65568 | tf_op jit(solution)/shard_map/ppermute | solution.py:273
  5.0 0.2 collective-permute-start.1
  5.1 3.8 %collective-permute-done.1.refs_0_ = f32[64,128]{1,0:T(8,128)S(1)} collective-permute-done((f32[64,128]{1,0:T(8,128)S(1)}, f32[64,128]{1,0:T(8,128)S(1)}, u32[]{:S(2)}, u32[]{:S(2)}) %collective-permute-start.1) | collective-permute-done | bytes 32800 | tf_op jit(solution)/shard_map/ppermute | solution.py:281
  9.0 0.1 shard_map.48
  9.1 2.7 %collective-permute-start.4 = (f32[8,128]{1,0:T(8,128)S(1)}, f32[8,128]{1,0:T(8,128)S(1)}, u32[]{:S(2)}, u32[]{:S(2)}) collective-permute-start(f32[8,128]{1,0:T(8,128)S(1)} %get-tuple-element.25), channel_id=1, source_target_pairs={{0,4},{1,5},{2,6},{3,7},{4,0},{5,1},{6,2},{7,3},{8,12},{9,13},{10,... | collective-permute-start | bytes 12296 | tf_op jit(solution)/shard_map/ppermute | solution.py:293
  11.8 0.0 collective-permute-start.5
  11.8 0.0 copy-done
  11.8 2.6 %shard_map.49 = (f32[256,16,1,128]{3,2,1,0:T(1,128)}, f32[16,256,128]{2,1,0:T(8,128)S(1)}, bf16[4,64,192]{2,1,0:T(8,128)(2,1)S(1)}) custom-call(f32[4096,128]{1,0:T(8,128)S(1)} %get-tuple-element.16.cot, f32[4,64,64]{2,1,0:T(8,128)S(1)} %copy-done, f32[16,128]{1,0:T(8,128)S(1)} %get-tuple-element.17.kappa, f32[64,128]{1,0:T(8,128)S(1)} %get-tuple-element.19.spread), custom_call_target="tpu_custom_call" | custom-call | flops 201326592 | bytes 4194304 | tf_op jit(solution)/shard_map/pallas_call | solution.py:17
  14.3 0.0 collective-permute-done.4.first_c
  14.3 1.9 %collective-permute-done.5.second_c = f32[8,128]{1,0:T(8,128)S(1)} collective-permute-done((f32[8,128]{1,0:T(8,128)S(1)}, f32[8,128]{1,0:T(8,128)S(1)}, u32[]{:S(2)}, u32[]{:S(2)}) %collective-permute-start.5) | collective-permute-done | bytes 4128 | tf_op jit(solution)/shard_map/ppermute | solution.py:292
  16.3 0.0 collective-permute-done.2.first
  16.3 0.0 collective-permute-done.3.second
  16.3 1.1 %shard_map.50 = f32[256,16,1,128]{3,2,1,0:T(1,128)} custom-call(f32[256,16,1,128]{3,2,1,0:T(1,128)} %get-tuple-element.20.started, f32[16,256,128]{2,1,0:T(8,128)S(1)} %get-tuple-element.21.stage, bf16[4,64,192]{2,1,0:T(8,128)(2,1)S(1)} %get-tuple-element.22.matrices, f32[256,128]{1,0:T(8,128)S(1)} %collective-permute-done.2.first, ...), custom_call_target="tpu_custom_call", output_to_operand_aliasing={{}: (0, {})} | custom-call | flops 524288 | bytes 524288 | tf_op jit(solution)/shard_map/pallas_call | solution.py:17
  (1 shorter events, 0.0 us)
Async XLA Ops:
  0.0 11.8 %copy-start = (f32[4,64,64]{2,1,0:T(8,128)S(1)}, f32[4,64,64]{2,1,0:T(8,128)}, u32[]{:S(2)}) copy-start(f32[4,64,64]{2,1,0:T(8,128)} %blocks.1) | copy-start | bytes 196612
  1.7 14.5 %collective-permute-start.2 = (f32[256,128]{1,0:T(8,128)S(1)}, f32[256,128]{1,0:T(8,128)S(1)}, u32[]{:S(2)}, u32[]{:S(2)}) collective-permute-start(f32[256,128]{1,0:T(8,128)S(1)} %get-tuple-element.23), channel_id=1, source_target_pairs={{0,4},{1,5},{2,6},{3,7},{4,0},{5,1},{6,2},{7,3},{8,12},{9,13},{10,... | collective-permute-start | bytes 393224 | tf_op jit(solution)/shard_map/ppermute | solution.py:274
  3.3 13.0 %collective-permute-start.3 = (f32[256,128]{1,0:T(8,128)S(1)}, f32[256,128]{1,0:T(8,128)S(1)}, u32[]{:S(2)}, u32[]{:S(2)}) collective-permute-start(f32[256,128]{1,0:T(8,128)S(1)} %get-tuple-element.24), channel_id=1, source_target_pairs={{0,1},{1,0},{2,3},{3,2},{4,8},{5,9},{6,10},{7,11},{8,4},{9,5},{10,... | collective-permute-start | bytes 393224 | tf_op jit(solution)/shard_map/ppermute | solution.py:282
  3.7 1.3 %collective-permute-start = (f32[128,128]{1,0:T(8,128)S(1)}, f32[128,128]{1,0:T(8,128)S(1)}, u32[]{:S(2)}, u32[]{:S(2)}) collective-permute-start(f32[128,128]{1,0:T(8,128)S(1)} %get-tuple-element.18.own), channel_id=1, source_target_pairs={{0,1},{1,0},{2,3},{3,2},{4,5},{5,4},{6,7},{7,6},{8,9},{9,8},{10,11... | collective-permute-start | bytes 196616 | tf_op jit(solution)/shard_map/ppermute | solution.py:273
  5.0 4.0 %collective-permute-start.1 = (f32[64,128]{1,0:T(8,128)S(1)}, f32[64,128]{1,0:T(8,128)S(1)}, u32[]{:S(2)}, u32[]{:S(2)}) collective-permute-start(f32[64,128]{1,0:T(8,128)S(1)} %shard_map.47), channel_id=1, source_target_pairs={{2,0},{3,1},{0,2},{1,3},{6,4},{7,5},{4,6},{5,7},{10,8},{11,9},{8,1... | collective-permute-start | bytes 98312 | tf_op jit(solution)/shard_map/ppermute | solution.py:281
  9.1 5.3 %collective-permute-start.4 = (f32[8,128]{1,0:T(8,128)S(1)}, f32[8,128]{1,0:T(8,128)S(1)}, u32[]{:S(2)}, u32[]{:S(2)}) collective-permute-start(f32[8,128]{1,0:T(8,128)S(1)} %get-tuple-element.25), channel_id=1, source_target_pairs={{0,4},{1,5},{2,6},{3,7},{4,0},{5,1},{6,2},{7,3},{8,12},{9,13},{10,... | collective-permute-start | bytes 12296 | tf_op jit(solution)/shard_map/ppermute | solution.py:293
  11.8 4.5 %collective-permute-start.5 = (f32[8,128]{1,0:T(8,128)S(1)}, f32[8,128]{1,0:T(8,128)S(1)}, u32[]{:S(2)}, u32[]{:S(2)}) collective-permute-start(f32[8,128]{1,0:T(8,128)S(1)} %get-tuple-element.26), channel_id=1, source_target_pairs={{0,1},{1,0},{2,3},{3,2},{4,8},{5,9},{6,10},{7,11},{8,4},{9,5},{10,... | collective-permute-start | bytes 12296 | tf_op jit(solution)/shard_map/ppermute | solution.py:292

commit v5 on v4

--- a/solution.py
+++ b/solution.py
@@ -10,7 +10,8 @@
 VMEM = pl.BlockSpec(memory_space=pltpu.VMEM)
 HBM = pl.BlockSpec(memory_space=pltpu.HBM)
 LIMIT = 16 * 1024 * 1024
-LATE = 1
+AHEAD = 1
+LATE = 0
 
 
 def call(body, outs, cost, *args, ins=None, out_specs=None, scratch=(), aliases=None):
@@ -137,84 +138,127 @@
         second[f : f + 1, :] = jnp.where(is_above, low, high)
 
 
-def writes(dims, stage, out, sems, late):
-    fields, levels, rows = dims
-    split = (fields - LATE) * levels
-    part = pl.ds(split, LATE * levels) if late else pl.ds(0, split)
-    return [
-        pltpu.make_async_copy(stage.at[x, part], out.at[part, x, 0], sems.at[x])
-        for x in range(1, rows - 1)
-        if LATE or not late
-    ]
-
-
-def main_kernel(dims, cot, blocks, kappa, spread, out, stage, matrices, sems):
+def writes(dims, chosen, stage, out, sem):
+    _, levels, rows = dims
+    part = pl.ds(chosen.start * levels, len(chosen) * levels)
+    for x in range(1, rows - 1):
+        pltpu.make_async_copy(stage.at[x, part], out.at[part, x, 0], sem).start()
+    inner = stage.at[pl.ds(1, rows - 2), part]
+    return pltpu.make_async_copy(inner, inner, sem)
+
+
+def groups(fields):
+    late = range(fields - LATE, fields)
+    return range(AHEAD), range(AHEAD, fields - 1), range(fields - 1, late.start), late
+
+
+def section(dims, f, matrix, cot, kappa, spread, store):
+    levels, rows = dims[1:]
+    columns = kappa.shape[1]
+    load = lambda x: cot[pl.ds(f * levels * rows + x, levels, stride=rows), :]
+    top = lax.broadcasted_iota(jnp.int32, (8, columns), 0) == 7
+    before, here = None, load(0)
+    here_w = here * kappa[0:1, :]
+    totals = []
+    for x in range(rows):
+        total = here * (1.0 - 4.0 * kappa[x : x + 1, :]) + across(here_w)
+        if before is not None:
+            total = total + before
+        before = here_w
+        if x + 1 < rows:
+            here = load(x + 1)
+            here_w = here * kappa[x + 1 : x + 2, :]
+            total = total + here_w
+        if spread is not None:
+            carry = jnp.where(top, spread[f * rows + x : f * rows + x + 1, :], 0.0)
+            total = jnp.concatenate([total[: levels - 8], total[levels - 8 :] + carry], axis=0)
+        totals.append(total)
+        if len(totals) < 2 and x + 1 < rows:
+            continue
+        result = product(matrix, jnp.concatenate(totals, axis=1))
+        for i in range(len(totals)):
+            store(x + 1 - len(totals) + i, result[:, i * columns : (i + 1) * columns])
+        totals = []
+
+
+def matrix_of(turned):
+    high, low = halves(turned)
+    return jnp.concatenate([high, high, low], axis=1)
+
+
+def ahead_kernel(dims, cot, blocks, kappa, stage):
+    levels = dims[1]
+    for f in range(AHEAD):
+
+        def store(x, value):
+            stage[x, f * levels : (f + 1) * levels] = value
+
+        section(dims, f, matrix_of(jnp.transpose(blocks[f])), cot, kappa, None, store)
+
+
+def main_kernel(dims, cot, blocks, kappa, spread, ahead, out, stage, matrices, last, sems):
     fields, levels, rows = dims
     columns = kappa.shape[1]
-    top = lax.broadcasted_iota(jnp.int32, (8, columns), 0) == 7
-    copies = writes(dims, stage, out, sems, False)
+    copies = []
     for f in range(fields):
-        high, low = halves(jnp.transpose(blocks[f]))
-        matrix = jnp.concatenate([high, high, low], axis=1)
+        own = slice(f * levels, (f + 1) * levels)
+        turned = jnp.transpose(blocks[f])
+        last[own, :] = jnp.broadcast_to(turned[:, levels - 1 :], (levels, columns))
+        matrix = matrix_of(turned)
         matrices[f] = matrix
-        load = lambda x: cot[pl.ds(f * levels * rows + x, levels, stride=rows), :]
-        before, here = None, load(0)
-        here_w = here * kappa[0:1, :]
-        totals = []
-        for x in range(rows):
-            total = here * (1.0 - 4.0 * kappa[x : x + 1, :]) + across(here_w)
-            if before is not None:
-                total = total + before
-            before = here_w
-            if x + 1 < rows:
-                here = load(x + 1)
-                here_w = here * kappa[x + 1 : x + 2, :]
-                total = total + here_w
-            carry = jnp.where(top, spread[f * rows + x : f * rows + x + 1, :], 0.0)
-            total = jnp.concatenate([total[: levels - 8], total[levels - 8 :] + carry], axis=0)
-            totals.append(total)
-            if len(totals) < 2 and x + 1 < rows:
-                continue
-            result = product(matrix, jnp.concatenate(totals, axis=1))
-            for i in range(len(totals)):
-                row = x + 1 - len(totals) + i
-                stage[row, f * levels : (f + 1) * levels] = result[:, i * columns : (i + 1) * columns]
-            totals = []
-        if f + 1 == fields - LATE:
-            for copy in copies:
-                copy.start()
+        if f < AHEAD:
+            for x in range(rows):
+                carry = spread[f * rows + x : f * rows + x + 1, :]
+                stage[x, own] = ahead[x, own] + last[own, :] * carry
+        else:
+
+            def store(x, value):
+                stage[x, own] = value
+
+            section(dims, f, matrix, cot, kappa, spread, store)
+        for i, group in enumerate(groups(fields)[:3]):
+            if f + 1 == group.stop and len(group):
+                copies.append(writes(dims, group, stage, out, sems.at[i]))
     for copy in copies:
         copy.wait()
 
 
+def halo_kernel(dims, strips, stage, matrices, first, second, edges):
+    fields, levels, rows = dims
+    columns = first.shape[1]
+    mine = lax.axis_index("strip")
+    is_above = first_is_above()
+    first_exists = jnp.where(is_above, mine + 1 < strips, mine > 0)
+    second_exists = jnp.where(is_above, mine > 0, mine + 1 < strips)
+    for f in range(fields):
+        at = slice(f * levels, (f + 1) * levels)
+        one = jnp.where(first_exists, first[at, :], 0.0)
+        two = jnp.where(second_exists, second[at, :], 0.0)
+        below = jnp.where(is_above, two, one)
+        above = jnp.where(is_above, one, two)
+        extra = product(matrices[f], jnp.concatenate([below, above], axis=1))
+        for side, x in ((0, 0), (1, rows - 1)):
+            edges[side, at] = stage[x, at] + extra[:, side * columns : (side + 1) * columns]
+
+
 def final_kernel(
-    dims, strips, started, stage, matrices, first, second, first_c, second_c, out, edges, sems
+    dims, strips, started, stage, partial, last, first, second, out, edges, sems
 ):
     fields, levels, rows = dims
-    columns = first.shape[1]
-    copies = writes(dims, stage, out, sems, True)
-    for copy in copies:
-        copy.start()
     mine = lax.axis_index("strip")
     is_above = first_is_above()
     below_exists, above_exists = mine > 0, mine + 1 < strips
-    top = lax.broadcasted_iota(jnp.int32, (8, columns), 0) == 7
-    for f in range(fields):
-        at = slice(f * levels, (f + 1) * levels)
-        sides = []
-        for halo, halo_c in ((first, first_c), (second, second_c)):
-            carry = jnp.where(top, halo_c[f : f + 1, :], 0.0)
-            value = halo[at, :]
-            sides.append(
-                jnp.concatenate([value[: levels - 8], value[levels - 8 :] + carry], axis=0)
-            )
-        below = jnp.where(below_exists, jnp.where(is_above, sides[1], sides[0]), 0.0)
-        above = jnp.where(above_exists, jnp.where(is_above, sides[0], sides[1]), 0.0)
-        extra = product(matrices[f], jnp.concatenate([below, above], axis=1))
-        for side, x in ((0, 0), (1, rows - 1)):
-            edges[side, at] = stage[x, at] + extra[:, side * columns : (side + 1) * columns]
+    late = groups(fields)[3]
+    copies = [writes(dims, late, stage, out, sems.at[2])] if len(late) else []
     for side, x in ((0, 0), (1, rows - 1)):
-        copies.append(pltpu.make_async_copy(edges.at[side], out.at[:, x, 0], sems.at[x]))
+        for f in range(fields):
+            row = slice(f, f + 1)
+            one, two = first[row, :], second[row, :]
+            below = jnp.where(below_exists, jnp.where(is_above, two, one), 0.0)
+            above = jnp.where(above_exists, jnp.where(is_above, one, two), 0.0)
+            at = slice(f * levels, (f + 1) * levels)
+            edges[side, at] = partial[side, at] + last[at, :] * (above if side else below)
+        copies.append(pltpu.make_async_copy(edges.at[side], out.at[:, x, 0], sems.at[side]))
         copies[-1].start()
     for copy in copies:
         copy.wait()
@@ -280,6 +324,14 @@
         moves = [(2 * s + c, 2 * i + c) for i, s in enumerate(sources(step, chips)) for c in range(2)]
         received.append(lax.ppermute(chip, "lev", moves))
     far = lax.ppermute(second, whole, two)
+    (ahead,) = call(
+        functools.partial(ahead_kernel, dims),
+        [f32(rows, AHEAD * levels, columns)],
+        (6 * levels * cot.size * AHEAD // fields, 2 * nbytes * AHEAD // fields),
+        held,
+        blocks,
+        kappa,
+    )
     spread, first, second = call(
         functools.partial(carry_kernel, dims, chips),
         [f32(size, columns), tiny, tiny],
@@ -291,33 +343,43 @@
     )
     far_c = lax.ppermute(second, whole, two)
     near_c = lax.ppermute(first, whole, one)
-    started, stage, matrices = call(
+    started, stage, matrices, last = call(
         functools.partial(main_kernel, dims),
-        [rowwise, by_row, wide],
+        [rowwise, by_row, wide, edge],
         (6 * levels * cot.size, 2 * nbytes),
         held,
         blocks,
         kappa,
         spread,
-        out_specs=[HBM, VMEM, VMEM],
-        scratch=[pltpu.SemaphoreType.DMA((rows,))],
-    )
-    (out,) = call(
-        functools.partial(final_kernel, dims, strips),
-        [rowwise],
-        (cot.size, nbytes // 4),
-        started,
+        ahead,
+        out_specs=[HBM, VMEM, VMEM, VMEM],
+        scratch=[pltpu.SemaphoreType.DMA((3,))],
+    )
+    sides = f32(2, fields * levels, columns)
+    (partial,) = call(
+        functools.partial(halo_kernel, dims, strips),
+        [sides],
+        (12 * levels * edge.size, 16 * edge.size),
         stage,
         matrices,
         near,
         far,
+    )
+    (out,) = call(
+        functools.partial(final_kernel, dims, strips),
+        [rowwise],
+        (4 * edge.size, 16 * edge.size),
+        started,
+        stage,
+        partial,
+        last,
         near_c,
         far_c,
-        ins=[HBM] + [VMEM] * 6,
+        ins=[HBM] + [VMEM] * 5,
         out_specs=[HBM],
         scratch=[
-            pltpu.VMEM((2, fields * levels, columns), jnp.float32),
-            pltpu.SemaphoreType.DMA((rows,)),
+            pltpu.VMEM(sides.shape, jnp.float32),
+            pltpu.SemaphoreType.DMA((3,)),
         ],
         aliases={0: 0},
     )

time: 17.5 us -> 17.2 us (0.983)
  waiting for transfers between devices: 7 us -> 6.55 us
    ppermute x1, waiting for transfers between devices: 3.83 us -> 3.25 us  [compute(): received.append(lax.ppermute(chip, 'lev', moves))]
    pallas_call x5 -> x7, Pallas kernels: 5.47 us -> 5.58 us  [call(): pl.pallas_call(body, out_shape=outs, in_specs=ins or [VMEM] * len(args),...]
  transfers between devices with their start and end apart: 6 -> 6, of which waited for: 3 -> 3; matrix products, arithmetic and copies ran while one was open for 0% -> 0% of each run, Pallas kernels for 15% -> 18%
where the time goes in v5:
time: 17.2 us; the launch traced here: 17 us
  waiting for transfers between devices  6.55 us (38%)
  Pallas kernels  5.58 us (32%)
  starting transfers between devices  4.82 us (28%)
    pallas_call x7, Pallas kernels, call(): pl.pallas_call(body, out_shape=outs, in_specs=ins or [VMEM] * len(args),...  5.58 us
    ppermute x1, waiting for transfers between devices, compute(): received.append(lax.ppermute(chip, 'lev', moves))  3.25 us
    ppermute x1, starting transfers between devices, compute(): near_c = lax.ppermute(first, whole, one)  2.68 us
    ppermute x1, waiting for transfers between devices, compute(): far_c = lax.ppermute(second, whole, two)  2.04 us
    ppermute x1, starting transfers between devices, compute(): near = lax.ppermute(first, whole, one)  1.56 us
    ppermute x1, waiting for transfers between devices, compute(): other = lax.ppermute(pair, 'lev', [(i, i ^ 1) for i in range(pieces)])  1.25 us
    ppermute x1, starting transfers between devices, compute(): far = lax.ppermute(second, whole, two)  0.42 us
  transfers between devices with their start and end apart: 6, of which 3 were waited for; matrix products, arithmetic and copies ran while one was open for 0% of the time, Pallas kernels for 18%

profile of v5, /device:TPU:12, one launch (start us, length us, event | category | flops | bytes accessed | tf_op | source)
XLA Modules:
  0.0 17.0 jit_solution(11136261408138323293)
XLA Ops:
  0.0 0.0 copy-start
  0.0 1.7 %shard_map.46 = (f32[4096,128]{1,0:T(8,128)S(1)}, f32[16,128]{1,0:T(8,128)S(1)}, f32[256,128]{1,0:T(8,128)S(1)}, f32[256,128]{1,0:T(8,128)S(1)}, f32[128,128]{1,0:T(8,128)S(1)}) custom-call(f32[4096,128]{1,0:T(8,128)} %bitcast.3, f32[64,128]{1,0:T(8,128)} %bitcast.4, f32[16,128]{1,0:T(8,128)} %kappa_hbm.1), custom_call_target="tpu_custom_call" | custom-call | flops 524288 | bytes 2097152 | tf_op jit(solution)/shard_map/pallas_call | solution.py:18
  1.7 1.6 %collective-permute-start.2 = (f32[256,128]{1,0:T(8,128)S(1)}, f32[256,128]{1,0:T(8,128)S(1)}, u32[]{:S(2)}, u32[]{:S(2)}) collective-permute-start(f32[256,128]{1,0:T(8,128)S(1)} %get-tuple-element.24), channel_id=1, source_target_pairs={{0,4},{1,5},{2,6},{3,7},{4,0},{5,1},{6,2},{7,3},{8,12},{9,13},{10,... | collective-permute-start | bytes 393224 | tf_op jit(solution)/shard_map/ppermute | solution.py:318
  3.3 0.4 %collective-permute-start.3 = (f32[256,128]{1,0:T(8,128)S(1)}, f32[256,128]{1,0:T(8,128)S(1)}, u32[]{:S(2)}, u32[]{:S(2)}) collective-permute-start(f32[256,128]{1,0:T(8,128)S(1)} %get-tuple-element.25), channel_id=1, source_target_pairs={{0,1},{1,0},{2,3},{3,2},{4,8},{5,9},{6,10},{7,11},{8,4},{9,5},{10,... | collective-permute-start | bytes 393224 | tf_op jit(solution)/shard_map/ppermute | solution.py:326
  3.7 0.0 collective-permute-start
  3.7 1.3 %collective-permute-done.other = f32[128,128]{1,0:T(8,128)S(1)} collective-permute-done((f32[128,128]{1,0:T(8,128)S(1)}, f32[128,128]{1,0:T(8,128)S(1)}, u32[]{:S(2)}, u32[]{:S(2)}) %collective-permute-start) | collective-permute-done | bytes 65568 | tf_op jit(solution)/shard_map/ppermute | solution.py:317
  5.0 0.2 collective-permute-start.1
  5.1 0.0 copy-done
  5.1 0.6 %shard_map.49.ahead = f32[16,64,128]{2,1,0:T(8,128)S(1)} custom-call(f32[4096,128]{1,0:T(8,128)S(1)} %get-tuple-element.17.cot, f32[4,64,64]{2,1,0:T(8,128)S(1)} %copy-done, f32[16,128]{1,0:T(8,128)S(1)} %get-tuple-element.18.kappa), custom_call_target="tpu_custom_call" | custom-call | flops 50331648 | bytes 1048576 | tf_op jit(solution)/shard_map/pallas_call | solution.py:18
  5.7 3.2 %collective-permute-done.1.refs_0_ = f32[64,128]{1,0:T(8,128)S(1)} collective-permute-done((f32[64,128]{1,0:T(8,128)S(1)}, f32[64,128]{1,0:T(8,128)S(1)}, u32[]{:S(2)}, u32[]{:S(2)}) %collective-permute-start.1) | collective-permute-done | bytes 32800 | tf_op jit(solution)/shard_map/ppermute | solution.py:325
  9.0 0.1 shard_map.48
  9.1 2.7 %collective-permute-start.4 = (f32[8,128]{1,0:T(8,128)S(1)}, f32[8,128]{1,0:T(8,128)S(1)}, u32[]{:S(2)}, u32[]{:S(2)}) collective-permute-start(f32[8,128]{1,0:T(8,128)S(1)} %get-tuple-element.27), channel_id=1, source_target_pairs={{0,4},{1,5},{2,6},{3,7},{4,0},{5,1},{6,2},{7,3},{8,12},{9,13},{10,... | collective-permute-start | bytes 12296 | tf_op jit(solution)/shard_map/ppermute | solution.py:345
  11.8 0.0 collective-permute-start.5
  11.8 2.2 %shard_map.50 = (f32[256,16,1,128]{3,2,1,0:T(1,128)}, f32[16,256,128]{2,1,0:T(8,128)S(1)}, bf16[4,64,192]{2,1,0:T(8,128)(2,1)S(1)}, f32[256,128]{1,0:T(8,128)S(1)}) custom-call(f32[4096,128]{1,0:T(8,128)S(1)} %get-tuple-element.17.cot, f32[4,64,64]{2,1,0:T(8,128)S(1)} %copy-done, f32[16,128]{1,0:T(8,128)S(1)} %get-tuple-element.18.kappa, ...), custom_call_target="tpu_custom_call" | custom-call | flops 201326592 | bytes 4194304 | tf_op jit(solution)/shard_map/pallas_call | solution.py:18
  14.0 0.0 collective-permute-done.2.first
  14.0 0.0 collective-permute-done.3.second
  14.0 0.2 %shard_map.51.partial = f32[2,256,128]{2,1,0:T(8,128)S(1)} custom-call(f32[16,256,128]{2,1,0:T(8,128)S(1)} %get-tuple-element.22.stage, bf16[4,64,192]{2,1,0:T(8,128)(2,1)S(1)} %get-tuple-element.23.matrices, f32[256,128]{1,0:T(8,128)S(1)} %collective-permute-done.2.first, f32[256,128]{1,0:T(8,128)S(1)} %collective-permute-done.3.second), custom_call_target="tpu_custom_call" | custom-call | flops 25165824 | bytes 524288 | tf_op jit(solution)/shard_map/pallas_call | solution.py:18
  14.2 0.0 collective-permute-done.4.first
  14.2 2.0 %collective-permute-done.5.second = f32[8,128]{1,0:T(8,128)S(1)} collective-permute-done((f32[8,128]{1,0:T(8,128)S(1)}, f32[8,128]{1,0:T(8,128)S(1)}, u32[]{:S(2)}, u32[]{:S(2)}) %collective-permute-start.5) | collective-permute-done | bytes 4128 | tf_op jit(solution)/shard_map/ppermute | solution.py:344
  16.3 0.7 %shard_map.52 = f32[256,16,1,128]{3,2,1,0:T(1,128)} custom-call(f32[256,16,1,128]{3,2,1,0:T(1,128)} %get-tuple-element.21.started, f32[16,256,128]{2,1,0:T(8,128)S(1)} %get-tuple-element.22.stage, f32[2,256,128]{2,1,0:T(8,128)S(1)} %shard_map.51.partial, f32[256,128]{1,0:T(8,128)S(1)} %get-tuple-element.26.last, ...), custom_call_target="tpu_custom_call", output_to_operand_aliasing={{}: (0, {})} | custom-call | flops 131072 | bytes 524288 | tf_op jit(solution)/shard_map/pallas_call | solution.py:18
  (1 shorter events, 0.0 us)
Async XLA Ops:
  0.0 5.1 %copy-start = (f32[4,64,64]{2,1,0:T(8,128)S(1)}, f32[4,64,64]{2,1,0:T(8,128)}, u32[]{:S(2)}) copy-start(f32[4,64,64]{2,1,0:T(8,128)} %blocks.3) | copy-start | bytes 196612
  1.7 12.2 %collective-permute-start.2 = (f32[256,128]{1,0:T(8,128)S(1)}, f32[256,128]{1,0:T(8,128)S(1)}, u32[]{:S(2)}, u32[]{:S(2)}) collective-permute-start(f32[256,128]{1,0:T(8,128)S(1)} %get-tuple-element.24), channel_id=1, source_target_pairs={{0,4},{1,5},{2,6},{3,7},{4,0},{5,1},{6,2},{7,3},{8,12},{9,13},{10,... | collective-permute-start | bytes 393224 | tf_op jit(solution)/shard_map/ppermute | solution.py:318
  3.3 10.7 %collective-permute-start.3 = (f32[256,128]{1,0:T(8,128)S(1)}, f32[256,128]{1,0:T(8,128)S(1)}, u32[]{:S(2)}, u32[]{:S(2)}) collective-permute-start(f32[256,128]{1,0:T(8,128)S(1)} %get-tuple-element.25), channel_id=1, source_target_pairs={{0,1},{1,0},{2,3},{3,2},{4,8},{5,9},{6,10},{7,11},{8,4},{9,5},{10,... | collective-permute-start | bytes 393224 | tf_op jit(solution)/shard_map/ppermute | solution.py:326
  3.7 1.3 %collective-permute-start = (f32[128,128]{1,0:T(8,128)S(1)}, f32[128,128]{1,0:T(8,128)S(1)}, u32[]{:S(2)}, u32[]{:S(2)}) collective-permute-start(f32[128,128]{1,0:T(8,128)S(1)} %get-tuple-element.19.own), channel_id=1, source_target_pairs={{0,1},{1,0},{2,3},{3,2},{4,5},{5,4},{6,7},{7,6},{8,9},{9,8},{10,11... | collective-permute-start | bytes 196616 | tf_op jit(solution)/shard_map/ppermute | solution.py:317
  5.0 4.0 %collective-permute-start.1 = (f32[64,128]{1,0:T(8,128)S(1)}, f32[64,128]{1,0:T(8,128)S(1)}, u32[]{:S(2)}, u32[]{:S(2)}) collective-permute-start(f32[64,128]{1,0:T(8,128)S(1)} %shard_map.47), channel_id=1, source_target_pairs={{2,0},{3,1},{0,2},{1,3},{6,4},{7,5},{4,6},{5,7},{10,8},{11,9},{8,1... | collective-permute-start | bytes 98312 | tf_op jit(solution)/shard_map/ppermute | solution.py:325
  9.1 5.1 %collective-permute-start.4 = (f32[8,128]{1,0:T(8,128)S(1)}, f32[8,128]{1,0:T(8,128)S(1)}, u32[]{:S(2)}, u32[]{:S(2)}) collective-permute-start(f32[8,128]{1,0:T(8,128)S(1)} %get-tuple-element.27), channel_id=1, source_target_pairs={{0,4},{1,5},{2,6},{3,7},{4,0},{5,1},{6,2},{7,3},{8,12},{9,13},{10,... | collective-permute-start | bytes 12296 | tf_op jit(solution)/shard_map/ppermute | solution.py:345
  11.8 4.5 %collective-permute-start.5 = (f32[8,128]{1,0:T(8,128)S(1)}, f32[8,128]{1,0:T(8,128)S(1)}, u32[]{:S(2)}, u32[]{:S(2)}) collective-permute-start(f32[8,128]{1,0:T(8,128)S(1)} %get-tuple-element.28), channel_id=1, source_target_pairs={{0,1},{1,0},{2,3},{3,2},{4,8},{5,9},{6,10},{7,11},{8,4},{9,5},{10,... | collective-permute-start | bytes 12296 | tf_op jit(solution)/shard_map/ppermute | solution.py:344

commit v6 on v5

--- a/solution.py
+++ b/solution.py
@@ -10,8 +10,7 @@
 VMEM = pl.BlockSpec(memory_space=pltpu.VMEM)
 HBM = pl.BlockSpec(memory_space=pltpu.HBM)
 LIMIT = 16 * 1024 * 1024
-AHEAD = 1
-LATE = 0
+AHEAD = (1, 2, 3)
 
 
 def call(body, outs, cost, *args, ins=None, out_specs=None, scratch=(), aliases=None):
@@ -139,17 +138,19 @@
 
 
 def writes(dims, chosen, stage, out, sem):
-    _, levels, rows = dims
+    levels, rows = dims[1:]
     part = pl.ds(chosen.start * levels, len(chosen) * levels)
     for x in range(1, rows - 1):
         pltpu.make_async_copy(stage.at[x, part], out.at[part, x, 0], sem).start()
-    inner = stage.at[pl.ds(1, rows - 2), part]
-    return pltpu.make_async_copy(inner, inner, sem)
+
+
+def landed(dims, chosen, stage):
+    levels, rows = dims[1:]
+    return stage.at[pl.ds(1, rows - 2), pl.ds(chosen.start * levels, len(chosen) * levels)]
 
 
 def groups(fields):
-    late = range(fields - LATE, fields)
-    return range(AHEAD), range(AHEAD, fields - 1), range(fields - 1, late.start), late
+    return range(1), range(1, fields - 1), range(fields - 1, fields)
 
 
 def section(dims, f, matrix, cot, kappa, spread, store):
@@ -186,41 +187,59 @@
     return jnp.concatenate([high, high, low], axis=1)
 
 
+def strip_kinds():
+    strip = lax.axis_index("strip")
+    odd = lax.rem(strip, 2) == 1
+    return odd, jnp.logical_and(jnp.logical_not(odd), strip > 0), strip == 0
+
+
 def ahead_kernel(dims, cot, blocks, kappa, stage):
-    levels = dims[1]
-    for f in range(AHEAD):
-
-        def store(x, value):
-            stage[x, f * levels : (f + 1) * levels] = value
-
-        section(dims, f, matrix_of(jnp.transpose(blocks[f])), cot, kappa, None, store)
+    fields, levels = dims[:2]
+
+    def run(chosen):
+        for f in chosen:
+
+            def store(x, value):
+                stage[x, f * levels : (f + 1) * levels] = value
+
+            section(dims, f, matrix_of(jnp.transpose(blocks[f])), cot, kappa, None, store)
+
+    run(range(AHEAD[0]))
+    for kind, count in list(zip(strip_kinds(), AHEAD))[1:]:
+        pl.when(kind)(functools.partial(run, range(AHEAD[0], min(count, fields))))
 
 
 def main_kernel(dims, cot, blocks, kappa, spread, ahead, out, stage, matrices, last, sems):
     fields, levels, rows = dims
     columns = kappa.shape[1]
-    copies = []
-    for f in range(fields):
-        own = slice(f * levels, (f + 1) * levels)
-        turned = jnp.transpose(blocks[f])
-        last[own, :] = jnp.broadcast_to(turned[:, levels - 1 :], (levels, columns))
-        matrix = matrix_of(turned)
-        matrices[f] = matrix
-        if f < AHEAD:
-            for x in range(rows):
-                carry = spread[f * rows + x : f * rows + x + 1, :]
-                stage[x, own] = ahead[x, own] + last[own, :] * carry
-        else:
-
-            def store(x, value):
-                stage[x, own] = value
-
-            section(dims, f, matrix, cot, kappa, spread, store)
-        for i, group in enumerate(groups(fields)[:3]):
-            if f + 1 == group.stop and len(group):
-                copies.append(writes(dims, group, stage, out, sems.at[i]))
-    for copy in copies:
-        copy.wait()
+
+    def run(done):
+        for f in range(fields):
+            own = slice(f * levels, (f + 1) * levels)
+            turned = jnp.transpose(blocks[f])
+            last[own, :] = jnp.broadcast_to(turned[:, levels - 1 :], (levels, columns))
+            matrix = matrix_of(turned)
+            matrices[f] = matrix
+            if f < done:
+                for x in range(rows):
+                    carry = spread[f * rows + x : f * rows + x + 1, :]
+                    stage[x, own] = ahead[x, own] + last[own, :] * carry
+            else:
+
+                def store(x, value):
+                    stage[x, own] = value
+
+                section(dims, f, matrix, cot, kappa, spread, store)
+            for i, group in enumerate(groups(fields)):
+                if f + 1 == group.stop and len(group):
+                    writes(dims, group, stage, out, sems.at[i])
+
+    for kind, count in zip(strip_kinds(), AHEAD):
+        pl.when(kind)(functools.partial(run, min(count, fields)))
+    for i, group in enumerate(groups(fields)):
+        if len(group):
+            inner = landed(dims, group, stage)
+            pltpu.make_async_copy(inner, inner, sems.at[i]).wait()
 
 
 def halo_kernel(dims, strips, stage, matrices, first, second, edges):
@@ -241,19 +260,16 @@
             edges[side, at] = stage[x, at] + extra[:, side * columns : (side + 1) * columns]
 
 
-def final_kernel(
-    dims, strips, started, stage, partial, last, first, second, out, edges, sems
-):
+def final_kernel(dims, strips, started, partial, last, first, inner, second, out, edges, sems):
     fields, levels, rows = dims
     mine = lax.axis_index("strip")
     is_above = first_is_above()
     below_exists, above_exists = mine > 0, mine + 1 < strips
-    late = groups(fields)[3]
-    copies = [writes(dims, late, stage, out, sems.at[2])] if len(late) else []
+    copies = []
     for side, x in ((0, 0), (1, rows - 1)):
         for f in range(fields):
             row = slice(f, f + 1)
-            one, two = first[row, :], second[row, :]
+            one, two = jnp.where(mine < 2, first[row, :], inner[row, :]), second[row, :]
             below = jnp.where(below_exists, jnp.where(is_above, two, one), 0.0)
             above = jnp.where(above_exists, jnp.where(is_above, one, two), 0.0)
             at = slice(f * levels, (f + 1) * levels)
@@ -276,13 +292,14 @@
     return [(i + step) % count for i in range(count)]
 
 
-def swaps(strips, pieces, turn):
+def swaps(strips, pieces, turn, chosen=None):
     pairs = []
     for strip in range(strips):
         other = ((strip + turn) ^ 1) - turn
         for piece in range(pieces):
             mine = strip * pieces + piece
             inside = 0 <= other < strips
+            inside = inside and strip in (chosen or range(strips))
             pairs.append((mine, other * pieces + piece if inside else mine ^ 1))
     return pairs
 
@@ -326,8 +343,8 @@
     far = lax.ppermute(second, whole, two)
     (ahead,) = call(
         functools.partial(ahead_kernel, dims),
-        [f32(rows, AHEAD * levels, columns)],
-        (6 * levels * cot.size * AHEAD // fields, 2 * nbytes * AHEAD // fields),
+        [f32(rows, min(AHEAD[-1], fields) * levels, columns)],
+        (6 * levels * cot.size * AHEAD[0] // fields, 2 * nbytes * AHEAD[0] // fields),
         held,
         blocks,
         kappa,
@@ -342,7 +359,8 @@
         *received,
     )
     far_c = lax.ppermute(second, whole, two)
-    near_c = lax.ppermute(first, whole, one)
+    near_c = lax.ppermute(first, whole, swaps(strips, pieces, 0, range(2)))
+    inner_c = lax.ppermute(first, whole, swaps(strips, pieces, 0, range(2, strips)))
     started, stage, matrices, last = call(
         functools.partial(main_kernel, dims),
         [rowwise, by_row, wide, edge],
@@ -370,16 +388,16 @@
         [rowwise],
         (4 * edge.size, 16 * edge.size),
         started,
-        stage,
         partial,
         last,
         near_c,
+        inner_c,
         far_c,
         ins=[HBM] + [VMEM] * 5,
         out_specs=[HBM],
         scratch=[
             pltpu.VMEM(sides.shape, jnp.float32),
-            pltpu.SemaphoreType.DMA((3,)),
+            pltpu.SemaphoreType.DMA((2,)),
         ],
         aliases={0: 0},
     )

time: 17.2 us -> 17.2 us (level)
  waiting for transfers between devices: 6.55 us -> 6.19 us
  Pallas kernels: 5.58 us -> 5.92 us
    ppermute x1, waiting for transfers between devices: 3.25 us -> 2.65 us  [compute(): received.append(lax.ppermute(chip, 'lev', moves))]
    pallas_call x7, Pallas kernels: 5.58 us -> 5.92 us  [call(): pl.pallas_call(body, out_shape=outs, in_specs=ins or [VMEM] * len(args),...]
    ppermute x1, waiting for transfers between devices: 2.04 us -> 2.27 us  [compute(): far_c = lax.ppermute(second, whole, two)]
    ppermute x1 -> x2, starting transfers between devices: 2.68 us -> 2.75 us  [the longest x1 2.68 us: compute(): lax.ppermute(first, whole, swaps(strips, pieces, 0, range(2, strips)))]
  transfers between devices with their start and end apart: 6 -> 7, of which waited for: 3 -> 3; matrix products, arithmetic and copies ran while one was open for 0% -> 0% of each run, Pallas kernels for 18% -> 20%
where the time goes in v6:
time: 17.2 us; the launch traced here: 17.1 us
  waiting for transfers between devices  6.19 us (36%)
  Pallas kernels  5.92 us (34%)
  starting transfers between devices  4.89 us (28%)
    pallas_call x7, Pallas kernels, call(): pl.pallas_call(body, out_shape=outs, in_specs=ins or [VMEM] * len(args),...  5.92 us
    ppermute x1, starting transfers between devices, compute(): lax.ppermute(first, whole, swaps(strips, pieces, 0, range(2, strips)))  2.68 us
    ppermute x1, waiting for transfers between devices, compute(): received.append(lax.ppermute(chip, 'lev', moves))  2.65 us
    ppermute x1, waiting for transfers between devices, compute(): far_c = lax.ppermute(second, whole, two)  2.27 us
    ppermute x1, starting transfers between devices, compute(): near = lax.ppermute(first, whole, one)  1.56 us
    ppermute x1, waiting for transfers between devices, compute(): other = lax.ppermute(pair, 'lev', [(i, i ^ 1) for i in range(pieces)])  1.25 us
    ppermute x1, starting transfers between devices, compute(): far = lax.ppermute(second, whole, two)  0.42 us
  transfers between devices with their start and end apart: 7, of which 3 were waited for; matrix products, arithmetic and copies ran while one was open for 0% of the time, Pallas kernels for 20%

profile of v6, /device:TPU:12, one launch (start us, length us, event | category | flops | bytes accessed | tf_op | source)
XLA Modules:
  0.0 17.1 jit_solution(4986258172426299779)
XLA Ops:
  0.0 0.0 copy-start
  0.0 1.7 %shard_map.46 = (f32[4096,128]{1,0:T(8,128)S(1)}, f32[16,128]{1,0:T(8,128)S(1)}, f32[256,128]{1,0:T(8,128)S(1)}, f32[256,128]{1,0:T(8,128)S(1)}, f32[128,128]{1,0:T(8,128)S(1)}) custom-call(f32[4096,128]{1,0:T(8,128)} %bitcast.3, f32[64,128]{1,0:T(8,128)} %bitcast.4, f32[16,128]{1,0:T(8,128)} %kappa_hbm.1), custom_call_target="tpu_custom_call" | custom-call | flops 524288 | bytes 2097152 | tf_op jit(solution)/shard_map/pallas_call | solution.py:17
  1.7 1.6 %collective-permute-start.2 = (f32[256,128]{1,0:T(8,128)S(1)}, f32[256,128]{1,0:T(8,128)S(1)}, u32[]{:S(2)}, u32[]{:S(2)}) collective-permute-start(f32[256,128]{1,0:T(8,128)S(1)} %get-tuple-element.24), channel_id=1, source_target_pairs={{0,4},{1,5},{2,6},{3,7},{4,0},{5,1},{6,2},{7,3},{8,12},{9,13},{10,... | collective-permute-start | bytes 393224 | tf_op jit(solution)/shard_map/ppermute | solution.py:335
  3.3 0.4 %collective-permute-start.3 = (f32[256,128]{1,0:T(8,128)S(1)}, f32[256,128]{1,0:T(8,128)S(1)}, u32[]{:S(2)}, u32[]{:S(2)}) collective-permute-start(f32[256,128]{1,0:T(8,128)S(1)} %get-tuple-element.25), channel_id=1, source_target_pairs={{0,1},{1,0},{2,3},{3,2},{4,8},{5,9},{6,10},{7,11},{8,4},{9,5},{10,... | collective-permute-start | bytes 393224 | tf_op jit(solution)/shard_map/ppermute | solution.py:343
  3.7 0.0 collective-permute-start
  3.7 1.3 %collective-permute-done.other = f32[128,128]{1,0:T(8,128)S(1)} collective-permute-done((f32[128,128]{1,0:T(8,128)S(1)}, f32[128,128]{1,0:T(8,128)S(1)}, u32[]{:S(2)}, u32[]{:S(2)}) %collective-permute-start) | collective-permute-done | bytes 65568 | tf_op jit(solution)/shard_map/ppermute | solution.py:334
  5.0 0.2 collective-permute-start.1
  5.1 0.0 copy-done
  5.1 1.2 %shard_map.49.ahead = f32[16,192,128]{2,1,0:T(8,128)S(1)} custom-call(f32[4096,128]{1,0:T(8,128)S(1)} %get-tuple-element.17.cot, f32[4,64,64]{2,1,0:T(8,128)S(1)} %copy-done, f32[16,128]{1,0:T(8,128)S(1)} %get-tuple-element.18.kappa), custom_call_target="tpu_custom_call" | custom-call | flops 50331648 | bytes 1048576 | tf_op jit(solution)/shard_map/pallas_call | solution.py:17
  6.3 2.7 %collective-permute-done.1.refs_0_ = f32[64,128]{1,0:T(8,128)S(1)} collective-permute-done((f32[64,128]{1,0:T(8,128)S(1)}, f32[64,128]{1,0:T(8,128)S(1)}, u32[]{:S(2)}, u32[]{:S(2)}) %collective-permute-start.1) | collective-permute-done | bytes 32800 | tf_op jit(solution)/shard_map/ppermute | solution.py:342
  9.0 0.1 shard_map.48
  9.1 0.1 collective-permute-start.4
  9.2 2.7 %collective-permute-start.5 = (f32[8,128]{1,0:T(8,128)S(1)}, f32[8,128]{1,0:T(8,128)S(1)}, u32[]{:S(2)}, u32[]{:S(2)}) collective-permute-start(f32[8,128]{1,0:T(8,128)S(1)} %get-tuple-element.27), channel_id=1, source_target_pairs={{0,1},{1,0},{2,3},{3,2},{4,5},{5,4},{6,7},{7,6},{8,12},{9,13},{10,... | collective-permute-start | bytes 12296 | tf_op jit(solution)/shard_map/ppermute | solution.py:363
  11.8 0.0 collective-permute-start.6
  11.8 2.0 %shard_map.50 = (f32[256,16,1,128]{3,2,1,0:T(1,128)}, f32[16,256,128]{2,1,0:T(8,128)S(1)}, bf16[4,64,192]{2,1,0:T(8,128)(2,1)S(1)}, f32[256,128]{1,0:T(8,128)S(1)}) custom-call(f32[4096,128]{1,0:T(8,128)S(1)} %get-tuple-element.17.cot, f32[4,64,64]{2,1,0:T(8,128)S(1)} %copy-done, f32[16,128]{1,0:T(8,128)S(1)} %get-tuple-element.18.kappa, ...), custom_call_target="tpu_custom_call" | custom-call | flops 201326592 | bytes 4194304 | tf_op jit(solution)/shard_map/pallas_call | solution.py:17
  13.8 0.0 collective-permute-done.2.first
  13.8 0.0 collective-permute-done.3.second
  13.8 0.2 %shard_map.51.partial = f32[2,256,128]{2,1,0:T(8,128)S(1)} custom-call(f32[16,256,128]{2,1,0:T(8,128)S(1)} %get-tuple-element.22.stage, bf16[4,64,192]{2,1,0:T(8,128)(2,1)S(1)} %get-tuple-element.23.matrices, f32[256,128]{1,0:T(8,128)S(1)} %collective-permute-done.2.first, f32[256,128]{1,0:T(8,128)S(1)} %collective-permute-done.3.second), custom_call_target="tpu_custom_call" | custom-call | flops 25165824 | bytes 524288 | tf_op jit(solution)/shard_map/pallas_call | solution.py:17
  14.0 0.0 collective-permute-done.4.first
  14.1 0.0 collective-permute-done.5.inner
  14.1 2.3 %collective-permute-done.6.second = f32[8,128]{1,0:T(8,128)S(1)} collective-permute-done((f32[8,128]{1,0:T(8,128)S(1)}, f32[8,128]{1,0:T(8,128)S(1)}, u32[]{:S(2)}, u32[]{:S(2)}) %collective-permute-start.6) | collective-permute-done | bytes 4128 | tf_op jit(solution)/shard_map/ppermute | solution.py:361
  16.3 0.7 %shard_map.52 = f32[256,16,1,128]{3,2,1,0:T(1,128)} custom-call(f32[256,16,1,128]{3,2,1,0:T(1,128)} %get-tuple-element.21.started, f32[2,256,128]{2,1,0:T(8,128)S(1)} %shard_map.51.partial, f32[256,128]{1,0:T(8,128)S(1)} %get-tuple-element.26.last, f32[8,128]{1,0:T(8,128)S(1)} %collective-permute-done.4.first, ...), custom_call_target="tpu_custom_call", output_to_operand_aliasing={{}: (0, {})} | custom-call | flops 131072 | bytes 524288 | tf_op jit(solution)/shard_map/pallas_call | solution.py:17
  (1 shorter events, 0.0 us)
Async XLA Ops:
  0.0 5.1 %copy-start = (f32[4,64,64]{2,1,0:T(8,128)S(1)}, f32[4,64,64]{2,1,0:T(8,128)}, u32[]{:S(2)}) copy-start(f32[4,64,64]{2,1,0:T(8,128)} %blocks.3) | copy-start | bytes 196612
  1.7 12.1 %collective-permute-start.2 = (f32[256,128]{1,0:T(8,128)S(1)}, f32[256,128]{1,0:T(8,128)S(1)}, u32[]{:S(2)}, u32[]{:S(2)}) collective-permute-start(f32[256,128]{1,0:T(8,128)S(1)} %get-tuple-element.24), channel_id=1, source_target_pairs={{0,4},{1,5},{2,6},{3,7},{4,0},{5,1},{6,2},{7,3},{8,12},{9,13},{10,... | collective-permute-start | bytes 393224 | tf_op jit(solution)/shard_map/ppermute | solution.py:335
  3.3 10.5 %collective-permute-start.3 = (f32[256,128]{1,0:T(8,128)S(1)}, f32[256,128]{1,0:T(8,128)S(1)}, u32[]{:S(2)}, u32[]{:S(2)}) collective-permute-start(f32[256,128]{1,0:T(8,128)S(1)} %get-tuple-element.25), channel_id=1, source_target_pairs={{0,1},{1,0},{2,3},{3,2},{4,8},{5,9},{6,10},{7,11},{8,4},{9,5},{10,... | collective-permute-start | bytes 393224 | tf_op jit(solution)/shard_map/ppermute | solution.py:343
  3.7 1.3 %collective-permute-start = (f32[128,128]{1,0:T(8,128)S(1)}, f32[128,128]{1,0:T(8,128)S(1)}, u32[]{:S(2)}, u32[]{:S(2)}) collective-permute-start(f32[128,128]{1,0:T(8,128)S(1)} %get-tuple-element.19.own), channel_id=1, source_target_pairs={{0,1},{1,0},{2,3},{3,2},{4,5},{5,4},{6,7},{7,6},{8,9},{9,8},{10,11... | collective-permute-start | bytes 196616 | tf_op jit(solution)/shard_map/ppermute | solution.py:334
  5.0 4.0 %collective-permute-start.1 = (f32[64,128]{1,0:T(8,128)S(1)}, f32[64,128]{1,0:T(8,128)S(1)}, u32[]{:S(2)}, u32[]{:S(2)}) collective-permute-start(f32[64,128]{1,0:T(8,128)S(1)} %shard_map.47), channel_id=1, source_target_pairs={{2,0},{3,1},{0,2},{1,3},{6,4},{7,5},{4,6},{5,7},{10,8},{11,9},{8,1... | collective-permute-start | bytes 98312 | tf_op jit(solution)/shard_map/ppermute | solution.py:342
  9.1 5.0 %collective-permute-start.4 = (f32[8,128]{1,0:T(8,128)S(1)}, f32[8,128]{1,0:T(8,128)S(1)}, u32[]{:S(2)}, u32[]{:S(2)}) collective-permute-start(f32[8,128]{1,0:T(8,128)S(1)} %get-tuple-element.27), channel_id=1, source_target_pairs={{0,4},{1,5},{2,6},{3,7},{4,0},{5,1},{6,2},{7,3},{8,9},{9,8},{10,11... | collective-permute-start | bytes 12296 | tf_op jit(solution)/shard_map/ppermute | solution.py:362
  9.2 4.9 %collective-permute-start.5 = (f32[8,128]{1,0:T(8,128)S(1)}, f32[8,128]{1,0:T(8,128)S(1)}, u32[]{:S(2)}, u32[]{:S(2)}) collective-permute-start(f32[8,128]{1,0:T(8,128)S(1)} %get-tuple-element.27), channel_id=1, source_target_pairs={{0,1},{1,0},{2,3},{3,2},{4,5},{5,4},{6,7},{7,6},{8,12},{9,13},{10,... | collective-permute-start | bytes 12296 | tf_op jit(solution)/shard_map/ppermute | solution.py:363
  11.8 4.5 %collective-permute-start.6 = (f32[8,128]{1,0:T(8,128)S(1)}, f32[8,128]{1,0:T(8,128)S(1)}, u32[]{:S(2)}, u32[]{:S(2)}) collective-permute-start(f32[8,128]{1,0:T(8,128)S(1)} %get-tuple-element.28), channel_id=1, source_target_pairs={{0,1},{1,0},{2,3},{3,2},{4,8},{5,9},{6,10},{7,11},{8,4},{9,5},{10,... | collective-permute-start | bytes 12296 | tf_op jit(solution)/shard_map/ppermute | solution.py:361
